TPU v7x, 32 devices: a whole 2x2x4 slice. The times are simulated.
32 devices in a mesh: row: 8 (over z, x), col: 4 (over y, core).
Axes of the slice: x: 2, y: 2, z: 4, core: 2. Of those that a mesh axis runs over, the one named last changes fastest.
Arguments:
- tokens: bfloat16 [4096, 768], P(('row', 'col')), may hold values from -6 to 6
- w_qkv: bfloat16 [768, 3, 768], P('row', None, 'col'), may hold values from -0.21875 to 0.21875
- w_out: bfloat16 [768, 768], P('col', 'row'), may hold values from -2.5 to 2.5
- w_gate_up: bfloat16 [768, 2, 3072], P('row', None, 'col'), may hold values from -0.21875 to 0.21875
- w_down: bfloat16 [3072, 768], P('col', 'row'), may hold values from -0.109375 to 0.109375
- gain1: float32 [768], replicated, may hold values from 0.1 to 1.9
- bias1: float32 [768], replicated, may hold values from -1.8 to 1.8
- gain2: float32 [768], replicated, may hold values from 0.1 to 1.9
- bias2: float32 [768], replicated, may hold values from -1.8 to 1.8
- cotangent: bfloat16 [4096, 768], P(('row', 'col')), may hold values from -6 to 6
- seq_lengths: int32 [3], replicated, may hold values from 512 to 2048, as said below
- packed_order: int32 [4096], replicated, may hold values from 0 to 4095, each once
Outputs:
- output: bfloat16 [4096, 768], P(('row', 'col'))
- grad_tokens: float32 [4096, 768], P(('row', 'col'))
- grad_w_qkv: float32 [768, 3, 768], P('row', None, 'col')
- grad_w_out: float32 [768, 768], P('col', 'row')
- grad_w_gate_up: float32 [768, 2, 3072], P('row', None, 'col')
- grad_w_down: float32 [3072, 768], P('col', 'row')
- grad_gain1: float32 [768], replicated
- grad_bias1: float32 [768], replicated
- grad_gain2: float32 [768], replicated
- grad_bias2: float32 [768], replicated
Inputs may be any that keep to these rules, and one draw needn't show every extreme that they name: `seq_lengths`: 3 lengths that sum to 4096; the longest is exactly 2048.
All inputs are finite; a program needn't handle non-finite values.
Results may differ from a plain program's by a relative error of at most 0.024.
Values may be sent and summed in bfloat16 or wider, within the bound.
No kernel may reach another device: no remote copies, remote signals or barrier semaphores. Data moves between devices by JAX's collectives and lax.ppermute only.
A program may use at most 512 MiB of HBM per device.

v0:
```python
import math

import jax
import jax.numpy as jnp
from jax import lax
from jax.sharding import PartitionSpec as P

HEAD = 64


ROPE_BASE = 1000.0
NORM_EPS = 1e-12
MASKED = -1e30


def token_layout(seq_lengths, packed_order):
    seq_ends = jnp.cumsum(seq_lengths)
    seq_starts = seq_ends - seq_lengths
    seq_id = jnp.sum((packed_order[:, None] >= seq_ends[None, :]).astype(jnp.int32), axis=1)
    member = seq_id[:, None] == jnp.arange(seq_lengths.shape[0], dtype=jnp.int32)[None, :]
    start_of = jnp.sum(jnp.where(member, seq_starts[None, :], 0), axis=1)
    return (seq_id, packed_order - start_of)


def rope_tables(positions, head):
    half = head // 2
    freqs = ROPE_BASE ** (-jnp.arange(half, dtype=jnp.float32) * 2.0 / head)
    angles = positions.astype(jnp.float32)[:, None] * freqs[None, :]
    return (jnp.cos(angles), jnp.sin(angles))


def rotate(field, cosine, sine):
    half = field.shape[-1] // 2
    first = field[..., :half]
    second = field[..., half:]
    cos_b = cosine[:, None, :]
    sin_b = sine[:, None, :]
    return jnp.concatenate(
        [first * cos_b - second * sin_b, second * cos_b + first * sin_b], axis=-1
    )


def rotate_back(field, cosine, sine):
    half = field.shape[-1] // 2
    first = field[..., :half]
    second = field[..., half:]
    cos_b = cosine[:, None, :]
    sin_b = sine[:, None, :]
    return jnp.concatenate(
        [first * cos_b + second * sin_b, second * cos_b - first * sin_b], axis=-1
    )


def norm_forward(values, gain, bias):
    centered = values - jnp.mean(values, axis=-1, keepdims=True)
    inverse = lax.rsqrt(jnp.mean(centered * centered, axis=-1, keepdims=True) + NORM_EPS)
    normed = centered * inverse
    return (normed * gain + bias, normed, inverse)


def norm_backward(grad_out, normed, inverse, gain):
    scaled = grad_out * gain
    grad_in = inverse * (
        scaled
        - jnp.mean(scaled, axis=-1, keepdims=True)
        - normed * jnp.mean(scaled * normed, axis=-1, keepdims=True)
    )
    return (grad_in, jnp.sum(grad_out * normed, axis=0), jnp.sum(grad_out, axis=0))


def gather_rows(rows):
    return lax.all_gather(rows, "col", axis=0, tiled=True)


def gather_grads(rows):
    return lax.all_gather(rows, "col", axis=0, tiled=True)


def column_sum(left, product):
    return lax.psum_scatter(
        product(left).astype(jnp.bfloat16), "col", scatter_dimension=0, tiled=True
    ).astype(jnp.float32)


def score_block(queries, seg_queries, key_rows, seg_keys, scale):
    count = key_rows.shape[0]
    heads = queries.shape[1]
    head = queries.shape[2]
    scores = (
        jnp.einsum(
            "qhd,khd->hqk",
            queries,
            key_rows.reshape(count, heads, head),
            preferred_element_type=jnp.float32,
        )
        * scale
    )
    same = seg_queries[:, None] == seg_keys[None, :]
    return (scores, same)


def probabilities(queries, seg_queries, log_total, key_rows, seg_keys, scale):
    scores, same = score_block(queries, seg_queries, key_rows, seg_keys, scale)
    return jnp.where(same[None], jnp.exp(scores - log_total[..., None]), 0.0)


def score_grads(probs, grad_heads, delta, value_rows):
    count = value_rows.shape[0]
    heads = grad_heads.shape[1]
    head = grad_heads.shape[2]
    grad_probs = jnp.einsum(
        "qhd,khd->hqk",
        grad_heads,
        value_rows.reshape(count, heads, head),
        preferred_element_type=jnp.float32,
    )
    return (probs * (grad_probs - delta[..., None])).astype(jnp.bfloat16)


def local(
    tokens,
    w_qkv,
    w_out,
    w_gate_up,
    w_down,
    gain1,
    bias1,
    gain2,
    bias2,
    cotangent,
    seq_lengths,
    packed_order,
):
    row_index = lax.axis_index("row")
    shards = lax.axis_size("row")
    full_qkv, full_out, full_gate_up, full_down = (
        lax.all_gather(w_qkv, "row", axis=0, tiled=True),
        lax.all_gather(w_out, "row", axis=1, tiled=True),
        lax.all_gather(w_gate_up, "row", axis=0, tiled=True),
        lax.all_gather(w_down, "row", axis=1, tiled=True),
    )
    seq_all, positions = token_layout(seq_lengths, packed_order)
    token_block = gather_rows(tokens)
    group = token_block.shape[0]
    first_slot = row_index * group
    seg_rows = lax.dynamic_slice_in_dim(seq_all, first_slot, group, 0)
    cosine, sine = rope_tables(lax.dynamic_slice_in_dim(positions, first_slot, group, 0), HEAD)
    width = full_qkv.shape[2]
    local_heads = width // HEAD
    scale = 1.0 / math.sqrt(HEAD)
    mixed = jnp.einsum("td,dce->tce", token_block, full_qkv, preferred_element_type=jnp.float32)
    query_bf = rotate(mixed[:, 0].reshape(group, local_heads, HEAD), cosine, sine).astype(
        jnp.bfloat16
    )
    key_bf = (
        rotate(mixed[:, 1].reshape(group, local_heads, HEAD), cosine, sine)
        .astype(jnp.bfloat16)
        .reshape(group, width)
    )
    value_bf = mixed[:, 2].astype(jnp.bfloat16)
    run_max = jnp.full((local_heads, group), MASKED, jnp.float32)
    key_piece = lax.all_gather(key_bf, "row", axis=0, tiled=True)
    value_piece = lax.all_gather(value_bf, "row", axis=0, tiled=True)
    count = key_piece.shape[0]
    seg_keys = seq_all
    scores, same = score_block(query_bf, seg_rows, key_piece, seg_keys, scale)
    new_max = jnp.maximum(run_max, jnp.max(jnp.where(same[None], scores, MASKED), axis=-1))
    weights_now = jnp.where(same[None], jnp.exp(scores - new_max[..., None]), 0.0)
    new_total = jnp.sum(weights_now, axis=-1)
    new_acc = jnp.einsum(
        "hqk,khd->hqd",
        weights_now.astype(jnp.bfloat16),
        value_piece.reshape(count, local_heads, HEAD),
        preferred_element_type=jnp.float32,
    )
    context = new_acc / new_total[..., None]
    log_total = new_max + jnp.log(new_total)
    context_bf = jnp.transpose(context, (1, 0, 2)).reshape(group, width).astype(jnp.bfloat16)

    def out_product(rows):
        return jnp.dot(rows, full_out, preferred_element_type=jnp.float32)

    attn_out = column_sum(context_bf, out_product)
    residual1 = tokens.astype(jnp.float32) + attn_out
    hidden1, normed1, inverse1 = norm_forward(residual1, gain1, bias1)
    hidden_block = gather_rows(hidden1.astype(jnp.bfloat16))
    gate_up = jnp.einsum(
        "td,dcf->tcf", hidden_block, full_gate_up, preferred_element_type=jnp.float32
    )
    up = gate_up[:, 0]
    gate = gate_up[:, 1]
    sigma = jax.nn.sigmoid(gate)
    inner = (gate * sigma * up).astype(jnp.bfloat16)

    def down_product(rows):
        return jnp.dot(rows, full_down, preferred_element_type=jnp.float32)

    ffn_out = column_sum(inner, down_product)
    residual2 = hidden1 + ffn_out
    result, normed2, inverse2 = norm_forward(residual2, gain2, bias2)
    grad_res2, grad_gain2, grad_bias2 = norm_backward(
        cotangent.astype(jnp.float32), normed2, inverse2, gain2
    )
    grad_ffn = gather_grads(grad_res2.astype(jnp.bfloat16))
    grad_inner = lax.dot_general(
        grad_ffn, full_down, (((1,), (1,)), ((), ())), preferred_element_type=jnp.float32
    )
    grad_down = lax.dot_general(
        inner, grad_ffn, (((0,), (0,)), ((), ())), preferred_element_type=jnp.float32
    )
    grad_up = grad_inner * gate * sigma
    grad_gate = grad_inner * up * sigma * (1.0 + gate * (1.0 - sigma))
    grad_gate_up = jnp.stack([grad_up, grad_gate], axis=1).astype(jnp.bfloat16)

    def gate_up_back(rows):
        return jnp.einsum("tcf,dcf->td", rows, full_gate_up, preferred_element_type=jnp.float32)

    grad_hidden1 = grad_res2 + column_sum(grad_gate_up, gate_up_back)
    grad_wgu = jnp.einsum(
        "td,tcf->dcf", hidden_block, grad_gate_up, preferred_element_type=jnp.float32
    )
    grad_res1, grad_gain1, grad_bias1 = norm_backward(grad_hidden1, normed1, inverse1, gain1)
    grad_attn = gather_grads(grad_res1.astype(jnp.bfloat16))
    grad_wo = lax.dot_general(
        context_bf, grad_attn, (((0,), (0,)), ((), ())), preferred_element_type=jnp.float32
    )
    grad_context_bf = lax.dot_general(
        grad_attn, full_out, (((1,), (1,)), ((), ())), preferred_element_type=jnp.float32
    ).astype(jnp.bfloat16)
    grad_heads = grad_context_bf.reshape(group, local_heads, HEAD)
    delta = jnp.sum(jnp.transpose(grad_heads, (1, 0, 2)).astype(jnp.float32) * context, axis=-1)
    key_all, value_all = (
        lax.all_gather(key_bf, "row", axis=0, tiled=True),
        lax.all_gather(value_bf, "row", axis=0, tiled=True),
    )
    tokens_total = key_all.shape[0]
    per_turn = group * math.gcd(shards, max(1, 2048 // group))
    turns = tokens_total // per_turn

    def turn_terms(turn):
        begin = turn * per_turn
        key_rows = lax.dynamic_slice_in_dim(key_all, begin, per_turn, 0)
        value_rows = lax.dynamic_slice_in_dim(value_all, begin, per_turn, 0)
        seg_keys = lax.dynamic_slice_in_dim(seq_all, begin, per_turn, 0)
        probs = probabilities(query_bf, seg_rows, log_total, key_rows, seg_keys, scale)
        grad_scores = score_grads(probs, grad_heads, delta, value_rows)
        return (begin, key_rows, probs, grad_scores)

    def query_term(grad_scores, key_rows):
        return jnp.einsum(
            "hqk,khd->qhd",
            grad_scores,
            key_rows.reshape(per_turn, local_heads, HEAD),
            preferred_element_type=jnp.float32,
        )

    empty_query = jnp.zeros((group, local_heads, HEAD), jnp.float32)

    def key_turn(turn, carry):
        grad_query, grad_keys, grad_values = carry
        begin, key_rows, probs, grad_scores = turn_terms(turn)
        grad_query = grad_query + query_term(grad_scores, key_rows)
        key_term = jnp.einsum(
            "hqk,qhd->khd", grad_scores, query_bf, preferred_element_type=jnp.float32
        ).reshape(per_turn, width)
        value_term = jnp.einsum(
            "hqk,qhd->khd",
            probs.astype(jnp.bfloat16),
            grad_heads,
            preferred_element_type=jnp.float32,
        ).reshape(per_turn, width)
        grad_keys = lax.dynamic_update_slice_in_dim(grad_keys, key_term, begin, 0)
        grad_values = lax.dynamic_update_slice_in_dim(grad_values, value_term, begin, 0)
        return (grad_query, grad_keys, grad_values)

    empty_keys = jnp.zeros((tokens_total, width), jnp.float32)
    grad_query, grad_keys_all, grad_values_all = lax.fori_loop(
        0, turns, key_turn, (empty_query, empty_keys, empty_keys)
    )
    grad_key_rows, grad_value_rows = (
        lax.psum_scatter(grad_keys_all, "row", scatter_dimension=0, tiled=True),
        lax.psum_scatter(grad_values_all, "row", scatter_dimension=0, tiled=True),
    )
    grad_query_raw = rotate_back(grad_query * scale, cosine, sine).reshape(group, width)
    grad_key_raw = rotate_back(
        grad_key_rows.reshape(group, local_heads, HEAD) * scale, cosine, sine
    ).reshape(group, width)
    grad_mixed = jnp.stack([grad_query_raw, grad_key_raw, grad_value_rows], axis=1).astype(
        jnp.bfloat16
    )

    def qkv_back(rows):
        return jnp.einsum("tce,dce->td", rows, full_qkv, preferred_element_type=jnp.float32)

    grad_tokens = grad_res1 + column_sum(grad_mixed, qkv_back)
    grad_wqkv = jnp.einsum(
        "td,tce->dce", token_block, grad_mixed, preferred_element_type=jnp.float32
    )
    grad_w_qkv, grad_w_out, grad_w_gate_up, grad_w_down = (
        lax.psum_scatter(grad_wqkv, "row", scatter_dimension=0, tiled=True),
        lax.psum_scatter(grad_wo, "row", scatter_dimension=1, tiled=True),
        lax.psum_scatter(grad_wgu, "row", scatter_dimension=0, tiled=True),
        lax.psum_scatter(grad_down, "row", scatter_dimension=1, tiled=True),
    )
    norm_gain1, norm_bias1, norm_gain2, norm_bias2 = lax.psum(
        (grad_gain1, grad_bias1, grad_gain2, grad_bias2), ("row", "col")
    )
    return (
        result.astype(jnp.bfloat16),
        grad_tokens,
        grad_w_qkv,
        grad_w_out,
        grad_w_gate_up,
        grad_w_down,
        norm_gain1,
        norm_bias1,
        norm_gain2,
        norm_bias2,
    )


def solution(mesh):
    placed = (
        P(("row", "col"), None),
        P("row", None, "col"),
        P("col", "row"),
        P("row", None, "col"),
        P("col", "row"),
        P(),
        P(),
        P(),
        P(),
        P(("row", "col"), None),
        P(),
        P(),
    )
    return jax.shard_map(
        local,
        mesh=mesh,
        in_specs=placed,
        out_specs=(
            P(("row", "col"), None),
            P(("row", "col"), None),
            P("row", None, "col"),
            P("col", "row"),
            P("row", None, "col"),
            P("col", "row"),
            P(),
            P(),
            P(),
            P(),
        ),
        check_vma=False,
    )
```

profile of v0, /device:TPU:0, one launch (start us, length us, event | category | flops | bytes accessed | tf_op | source)
XLA Modules:
  0.0 918.4 jit_solution(15256059629411682818)
XLA Ops:
  8.8 1.0 copy.45
  9.8 38.8 %all_gather.33 = bf16[768,3,192]{2,1,0:T(4,128)(2,1)S(1)} all-gather(bf16[96,3,192]{2,1,0:T(4,128)(2,1)S(1)} %copy.45), channel_id=1, replica_groups=mesh['row'=8,'col'=4] {'row'}, dimensions={0}, use_global_device_ids=true | all-gather | bytes 995328 | tf_op jit(solution)/shard_map/all_gather | solution.py:137
  49.5 8.8 all_gather.32
  62.9 1.3 broadcast_compare_fusion.1
  64.3 31.8 %all_gather.36 = bf16[192,768]{0,1:T(8,128)(2,1)S(1)} all-gather(bf16[192,96]{0,1:T(8,128)(2,1)S(1)} %copy.47), channel_id=1, replica_groups=mesh['row'=8,'col'=4] {'row'}, dimensions={1}, use_global_device_ids=true | all-gather | bytes 331776 | tf_op jit(solution)/shard_map/all_gather | solution.py:138
  96.1 11.8 %all-gather.6.cloned.1.call-done = bf16[4096,192]{0,1:T(8,128)(2,1)} async-done(((bf16[512,192]{0,1:T(8,128)(2,1)}), bf16[4096,192]{0,1:T(8,128)(2,1)}) %all-gather.6.cloned.1.call-update) | async-done | bytes 1572880 | tf_op jit(solution)/shard_map/all_gather | solution.py:162
  107.9 12.5 %select_reduce_fusion = (f32[3,512]{1,0:T(4,128)S(1)}, f32[3,512,4096]{2,1,0:T(8,128)}) fusion(pred[512,4096]{1,0:T(8,128)(4,1)S(1)} %broadcast_compare_fusion.1, bf16[4096,3,64]{0,2,1:T(8,128)(2,1)} %bitcast.162, bf16[512,3,32]{0,2,1:T(8,128)(2,1)S(1)} %get-tuple-element.336, bf16[512,3,32]{0,2,1:T(8,128)(2,1)S(1)} %get-tuple-element.335), kind=kOutput, calls=%fused_computation.16 | convolution fusion | flops 824572416 | bytes 29038592 | tf_op jit(solution)/shard_map/qhd,khd->hqk/dot_general | solution.py:90
  120.4 12.0 %fusion.8 = f32[3,512]{1,0:T(4,128)S(1)} fusion(f32[3,512,4096]{2,1,0:T(8,128)} %get-tuple-element.347, f32[3,512]{1,0:T(4,128)S(1)} %broadcast_maximum_fusion, pred[512,4096]{1,0:T(8,128)(4,1)S(1)} %broadcast_compare_fusion.1), kind=kLoop, calls=%fused_computation.17 | loop fusion | flops 25164288 | bytes 27275264 | tf_op jit(solution)/shard_map/reduce_sum | solution.py:169
  132.4 21.2 %all-gather.12.cloned.1.call-done = bf16[4096,1,192]{0,2,1:T(8,128)(2,1)} async-done(((bf16[512,1,192]{0,2,1:T(8,128)(2,1)}), bf16[4096,1,192]{0,2,1:T(8,128)(2,1)}) %all-gather.12.cloned.1.call-update) | async-done | bytes 1572880 | tf_op jit(solution)/shard_map/all_gather | solution.py:163
  153.6 12.0 %fusion.29 = (bf16[512,3,64]{0,2,1:T(8,128)(2,1)S(1)}, f32[3,512,64]{1,2,0:T(8,128)}) fusion(f32[512,3]{0,1:T(4,128)S(1)} %bitcast.183, bf16[4096,3,64]{0,2,1:T(8,128)(2,1)} %bitcast.163, f32[3,512,4096]{2,1,0:T(8,128)} %get-tuple-element.347, f32[3,512]{1,0:T(4,128)S(1)} %broadcast_maximum_fusion, pred[512,4096]{1,0:T(8,128)(4,1)S(1)} %broadcast_compare_fusion.1), kind=kOutput, calls=%fused_computation.58 | convolution fusion | flops 830668800 | bytes 29437952 | tf_op jit(solution)/shard_map/hqk,khd->hqd/dot_general | solution.py:170
  165.6 1.3 convolution_convert_fusion.1
  167.0 1.7 copy.48
  169.4 19.2 %reduce-scatter.15.cloned.1.call-done = bf16[128,768]{1,0:T(8,128)(2,1)} async-done(((bf16[512,768]{1,0:T(8,128)(2,1)}), bf16[128,768]{1,0:T(8,128)(2,1)}) %reduce-scatter.15.cloned.1.call-update) | async-done | bytes 196624 | tf_op jit(solution)/shard_map/reduce_scatter | solution.py:80
  188.6 1.1 fusion.31
  189.6 1.1 multiply_reduce_fusion.3
  190.8 1.1 fusion.33
  191.8 8.4 all_gather.37
  200.2 43.2 %all-gather.8.cloned.1.call-done = bf16[768,2,768]{2,0,1:T(8,128)(2,1)} async-done(((bf16[96,2,768]{2,0,1:T(8,128)(2,1)}), bf16[768,2,768]{2,0,1:T(8,128)(2,1)}) %all-gather.8.cloned.1.call-update) | async-done | bytes 2359312 | tf_op jit(solution)/shard_map/all_gather | solution.py:139
  243.4 3.0 fusion.17
  246.5 1.6 copy-done.11
  248.6 36.7 %all-gather.10.cloned.1.call-done = bf16[768,768]{0,1:T(8,128)(2,1)} async-done(((bf16[768,96]{0,1:T(8,128)(2,1)}), bf16[768,768]{0,1:T(8,128)(2,1)}) %all-gather.10.cloned.1.call-update) | async-done | bytes 1179664 | tf_op jit(solution)/shard_map/all_gather | solution.py:140
  285.3 3.0 convolution_convert_fusion
  288.3 22.1 %reduce-scatter.17.cloned.1.call-done = bf16[128,768]{1,0:T(8,128)(2,1)} async-done(((bf16[512,768]{1,0:T(8,128)(2,1)}), bf16[128,768]{1,0:T(8,128)(2,1)}) %reduce-scatter.17.cloned.1.call-update) | async-done | bytes 196624 | tf_op jit(solution)/shard_map/reduce_scatter | solution.py:80
  310.5 1.3 fusion.46
  313.7 8.2 all_gather.40
  321.9 2.7 fusion.19
  325.8 2.3 bitcast_convert_fusion.1
  328.2 23.7 %reduce-scatter.19.cloned.1.call-done = bf16[128,768]{1,0:T(8,128)(2,1)} async-done(((bf16[512,768]{1,0:T(8,128)(2,1)}), bf16[128,768]{1,0:T(8,128)(2,1)}) %reduce-scatter.19.cloned.1.call-update) | async-done | bytes 196624 | tf_op jit(solution)/shard_map/reduce_scatter | solution.py:80
  352.0 1.2 multiply_reduce_fusion
  353.2 1.9 fusion.43
  355.1 8.2 all_gather.41
  364.2 2.0 broadcast_in_dim.122
  366.2 2.0 broadcast_in_dim.122.clone
  368.2 58.9 %while.18 = (s32[]{:T(128)}, f32[512,3,64]{0,2,1:T(8,128)S(1)}, f32[4096,192]{0,1:T(8,128)}, f32[4096,192]{0,1:T(8,128)}, bf16[4096,192]{0,1:T(8,128)(2,1)S(1)},...) while((s32[]{:T(128)}, f32[512,3,64]{0,2,1:T(8,128)S(1)}, ...), condition=%wide.region_18.19_spmd.clone, body=%wide.region_17.18_spmd.clone.sunk | while | flops 2045968384 | bytes 107786520 | solution.py:277
  368.3 6.4 fusion.105
  375.5 7.4 fusion.106
  382.9 2.0 fusion.109
  385.5 6.1 fusion.108
  391.6 2.1 constant_dynamic-update-slice_fusion.3
  393.6 4.0 fusion.107
  397.8 6.4 fusion.105
  404.9 7.4 fusion.106
  412.3 2.0 fusion.109
  414.9 6.1 fusion.108
  421.0 2.1 constant_dynamic-update-slice_fusion.3
  423.1 4.0 fusion.107
  428.3 1.4 convolution_bitcast_fusion.1
  429.8 4.7 fusion.13
  434.6 68.0 %reduce-scatter.21.cloned.1.call-done = f32[512,192]{0,1:T(8,128)} async-done(((f32[4096,192]{0,1:T(8,128)}), f32[512,192]{0,1:T(8,128)}) %reduce-scatter.21.cloned.1.call-update) | async-done | bytes 393232 | tf_op jit(solution)/shard_map/reduce_scatter | solution.py:281
  503.8 76.9 %reduce-scatter.23.cloned.1.call-done = f32[512,192]{0,1:T(8,128)} async-done(((f32[4096,192]{0,1:T(8,128)}), f32[512,192]{0,1:T(8,128)}) %reduce-scatter.23.cloned.1.call-update) | async-done | bytes 393232 | tf_op jit(solution)/shard_map/reduce_scatter | solution.py:282
  582.4 1.7 bitcast_convert_fusion
  584.5 1.7 fusion.14
  586.2 1.8 copy.62
  588.2 2.3 fusion.51
  590.5 40.1 %all-reduce = (f32[768]{0:T(1024)}, f32[768]{0:T(1024)}, f32[768]{0:T(1024)}, f32[768]{0:T(1024)}) all-reduce(f32[768]{0:T(1024)S(1)} %get-tuple-element.283, f32[768]{0:T(1024)S(1)} %get-tuple-element.288, f32[768]{0:T(1024)S(1)} %copy-done.34, f32[768]{0:T(1024)S(1)} %copy-done.35), channel_id=1, replica_groups=mesh['row'=8,'col'=4] {'row','col'}, use_global_device_ids=true, to_apply=%region_27.28 | all-reduce | flops 3072 | bytes 24576 | tf_op jit(solution)/shard_map/psum | solution.py:305
  630.6 15.3 %reduce-scatter.33.cloned.1.call-done = f32[96,192]{1,0:T(8,128)} async-done(((f32[768,192]{1,0:T(8,128)}), f32[96,192]{1,0:T(8,128)}) %reduce-scatter.33.cloned.1.call-update) | async-done | bytes 73744
  645.9 1.6 copy.61
  647.6 96.2 %reduce-scatter.27.cloned.1.call-done = f32[96,2,768]{2,0,1:T(8,128)} async-done(((f32[768,2,768]{2,0,1:T(8,128)}), f32[96,2,768]{2,0,1:T(8,128)}) %reduce-scatter.27.cloned.1.call-update) | async-done | bytes 589840 | tf_op jit(solution)/shard_map/reduce_scatter | solution.py:302
  743.8 2.3 copy.52
  746.1 23.1 %reduce-scatter.25.cloned.1.call-done = bf16[128,768]{1,0:T(8,128)(2,1)} async-done(((bf16[512,768]{1,0:T(8,128)(2,1)}), bf16[128,768]{1,0:T(8,128)(2,1)}) %reduce-scatter.25.cloned.1.call-update) | async-done | bytes 196624 | tf_op jit(solution)/shard_map/reduce_scatter | solution.py:80
  769.3 1.7 convert_add_fusion
  771.0 69.1 %reduce-scatter.31.cloned.1.call-done = f32[96,576]{1,0:T(8,128)} async-done(((f32[768,576]{1,0:T(8,128)}), f32[96,576]{1,0:T(8,128)}) %reduce-scatter.31.cloned.1.call-update) | async-done | bytes 221200
  840.0 1.1 copy.63
  842.0 69.8 %reduce-scatter.29.cloned.1.call-done = f32[768,96]{0,1:T(8,128)} async-done(((f32[768,768]{0,1:T(8,128)}), f32[768,96]{0,1:T(8,128)}) %reduce-scatter.29.cloned.1.call-update) | async-done | bytes 294928 | tf_op jit(solution)/shard_map/reduce_scatter | solution.py:303
  (160 shorter events, 20.6 us)
Async XLA Ops:
  7.2 42.3 %copy-start.3 = (bf16[128,768]{1,0:T(8,128)(2,1)S(1)}, bf16[128,768]{1,0:T(8,128)(2,1)}, u32[]{:S(2)}) copy-start(bf16[128,768]{1,0:T(8,128)(2,1)} %param.14) | copy-start | bytes 589828
  7.2 100.7 %all-gather.6.cloned.1.call-start = ((), (), s32[]{:S(2)}) async-start(), calls=%async_computation.10 | async-start | bytes 1769472 | tf_op jit(solution)/shard_map/all_gather | solution.py:162
  49.5 11.2 %copy-start.9 = (bf16[768,3,192]{0,2,1:T(8,128)(2,1)}, bf16[768,3,192]{0,2,1:T(8,128)(2,1)S(1)}, u32[]{:S(2)}) copy-start(bf16[768,3,192]{0,2,1:T(8,128)(2,1)S(1)} %copy.46) | copy-start | bytes 2654212
  49.5 10.4 %copy-start.31 = (s32[4096]{0:T(1024)S(1)}, s32[4096]{0:T(1024)}, u32[]{:S(2)}) copy-start(s32[4096]{0:T(1024)} %param.25) | copy-start | bytes 49156
  58.3 0.9 copy-start.13
  59.9 4.3 copy-start.30
  60.6 0.6 copy-start.21
  60.6 0.6 copy-start.23
  62.0 91.6 %all-gather.12.cloned.1.call-start = ((), (), s32[]{:S(2)}) async-start(), calls=%async_computation.21 | async-start | bytes 1769472 | tf_op jit(solution)/shard_map/all_gather | solution.py:163
  62.7 125.8 %reduce-scatter.15.cloned.1.call-start = ((), (), s32[]{:S(2)}) async-start(), calls=%async_computation.11 | async-start | bytes 983040 | tf_op jit(solution)/shard_map/reduce_scatter | solution.py:80
  165.6 25.1 %copy-start.29 = (f32[768]{0:T(1024)S(1)}, f32[768]{0:T(1024)}, u32[]{:S(2)}) copy-start(f32[768]{0:T(1024)} %param.19) | copy-start | bytes 9220
  165.6 25.1 %copy-start.32 = (f32[768]{0:T(1024)S(1)}, f32[768]{0:T(1024)}, u32[]{:S(2)}) copy-start(f32[768]{0:T(1024)} %param.20) | copy-start | bytes 9220
  167.0 76.4 %all-gather.8.cloned.1.call-start = ((), (), s32[]{:S(2)}) async-start(), calls=%async_computation.12 | async-start | bytes 2654208 | tf_op jit(solution)/shard_map/all_gather | solution.py:139
  168.8 116.5 %all-gather.10.cloned.1.call-start = ((), (), s32[]{:S(2)}) async-start(), calls=%async_computation.13 | async-start | bytes 1327104 | tf_op jit(solution)/shard_map/all_gather | solution.py:140
  169.3 141.1 %reduce-scatter.17.cloned.1.call-start = ((), (), s32[]{:S(2)}) async-start(), calls=%async_computation.14 | async-start | bytes 983040 | tf_op jit(solution)/shard_map/reduce_scatter | solution.py:80
  200.2 43.2 %copy-start.18 = (bf16[512,768]{1,0:T(8,128)(2,1)}, bf16[512,768]{1,0:T(8,128)(2,1)S(1)}, u32[]{:S(2)}) copy-start(bf16[512,768]{1,0:T(8,128)(2,1)S(1)} %all_gather.37) | copy-start | bytes 2359300
  246.5 1.6 copy-start.11
  248.6 64.2 %copy-start.7 = (bf16[512,768]{1,0:T(8,128)(2,1)}, bf16[512,768]{1,0:T(8,128)(2,1)S(1)}, u32[]{:S(2)}) copy-start(bf16[512,768]{1,0:T(8,128)(2,1)S(1)} %multiply_convert_fusion.2) | copy-start | bytes 2359300
  248.6 61.9 %copy-start.6 = (bf16[128,768]{1,0:T(8,128)(2,1)S(1)}, bf16[128,768]{1,0:T(8,128)(2,1)}, u32[]{:S(2)}) copy-start(bf16[128,768]{1,0:T(8,128)(2,1)} %reduce-scatter.15.cloned.1.call-done) | copy-start | bytes 589828
  248.6 63.4 %copy-start.20 = (bf16[128,768]{1,0:T(8,128)(2,1)S(1)}, bf16[128,768]{1,0:T(8,128)(2,1)}, u32[]{:S(2)}) copy-start(bf16[128,768]{1,0:T(8,128)(2,1)} %param.23) | copy-start | bytes 589828
  248.6 63.4 %copy-start.33 = (f32[768]{0:T(1024)S(1)}, f32[768]{0:T(1024)}, u32[]{:S(2)}) copy-start(f32[768]{0:T(1024)} %param.21) | copy-start | bytes 9220
  248.6 64.2 %copy-start.36 = (f32[768]{0:T(1024)S(1)}, f32[768]{0:T(1024)}, u32[]{:S(2)}) copy-start(f32[768]{0:T(1024)} %param.22) | copy-start | bytes 9220
  288.3 63.7 %reduce-scatter.19.cloned.1.call-start = ((), (), s32[]{:S(2)}) async-start(), calls=%async_computation.15 | async-start | bytes 983040 | tf_op jit(solution)/shard_map/reduce_scatter | solution.py:80
  310.5 11.4 %copy-start.12 = (f32[512,2,768]{2,0,1:T(8,128)S(1)}, f32[512,2,768]{2,0,1:T(8,128)}, u32[]{:S(2)}) copy-start(f32[512,2,768]{2,0,1:T(8,128)} %copy-done.11) | copy-start | bytes 9437188
  321.9 2.7 copy-start.15
  321.9 3.9 copy-start.37
  324.6 0.9 copy-start.38
  324.7 1.1 copy-start.40
  328.1 35.6 %copy-start.25 = (f32[3,512,64]{1,2,0:T(8,128)S(1)}, f32[3,512,64]{1,2,0:T(8,128)}, u32[]{:S(2)}) copy-start(f32[3,512,64]{1,2,0:T(8,128)} %get-tuple-element.349) | copy-start | bytes 1179652
  328.1 174.4 %reduce-scatter.21.cloned.1.call-start = ((), (), s32[]{:S(2)}) async-start(), calls=%async_computation.16 | async-start | bytes 3538944 | tf_op jit(solution)/shard_map/reduce_scatter | solution.py:281
  363.3 0.9 copy-start.4
  364.2 4.0 copy-start.1
  368.3 7.1 copy-start.2
  382.9 2.6 copy-start
  397.7 7.1 copy-start.2
  412.3 2.6 copy-start
  427.1 1.1 copy-start.5
  427.2 2.6 copy-start.19
  427.2 2.6 copy-start.39
  427.2 153.5 %reduce-scatter.23.cloned.1.call-start = ((), (), s32[]{:S(2)}) async-start(), calls=%async_computation.17 | async-start | bytes 3538944 | tf_op jit(solution)/shard_map/reduce_scatter | solution.py:282
  427.9 218.0 %reduce-scatter.33.cloned.1.call-start = ((), (), s32[]{:S(2)}) async-start(), calls=%async_computation.23 | async-start | bytes 884736
  429.7 314.1 %reduce-scatter.27.cloned.1.call-start = ((), (), s32[]{:S(2)}) async-start(), calls=%async_computation.19 | async-start | bytes 5308416 | tf_op jit(solution)/shard_map/reduce_scatter | solution.py:302
  434.5 69.1 %copy-start.22 = (f32[512,32]{0,1:T(8,128)S(1)}, f32[512,32]{0,1:T(8,128)}, u32[]{:S(2)}) copy-start(f32[512,32]{0,1:T(8,128)} %copy-done.21) | copy-start | bytes 196612
  434.5 69.1 %copy-start.24 = (f32[512,32]{0,1:T(8,128)S(1)}, f32[512,32]{0,1:T(8,128)}, u32[]{:S(2)}) copy-start(f32[512,32]{0,1:T(8,128)} %copy-done.23) | copy-start | bytes 196612
  434.5 147.9 %copy-start.10 = (bf16[768,3,192]{0,2,1:T(8,128)(2,1)S(1)}, bf16[768,3,192]{0,2,1:T(8,128)(2,1)}, u32[]{:S(2)}) copy-start(bf16[768,3,192]{0,2,1:T(8,128)(2,1)} %copy-done.9) | copy-start | bytes 2654212
  434.5 334.8 %reduce-scatter.25.cloned.1.call-start = ((), (), s32[]{:S(2)}) async-start(), calls=%async_computation.18 | async-start | bytes 983040 | tf_op jit(solution)/shard_map/reduce_scatter | solution.py:80
  503.7 80.4 %copy-start.26 = (bf16[512,3,64]{0,2,1:T(8,128)(2,1)}, bf16[512,3,64]{0,2,1:T(8,128)(2,1)S(1)}, u32[]{:S(2)}) copy-start(bf16[512,3,64]{0,2,1:T(8,128)(2,1)S(1)} %pad_maximum_fusion.8) | copy-start | bytes 589828
  503.8 80.7 %copy-start.14 = (bf16[512,768]{1,0:T(8,128)(2,1)S(1)}, bf16[512,768]{1,0:T(8,128)(2,1)}, u32[]{:S(2)}) copy-start(bf16[512,768]{1,0:T(8,128)(2,1)} %copy-done.13) | copy-start | bytes 2359300
  503.8 80.4 %copy-start.27 = (bf16[512,3,64]{0,2,1:T(8,128)(2,1)}, bf16[512,3,64]{0,2,1:T(8,128)(2,1)S(1)}, u32[]{:S(2)}) copy-start(bf16[512,3,64]{0,2,1:T(8,128)(2,1)S(1)} %pad_maximum_fusion.9) | copy-start | bytes 589828
  581.7 0.7 copy-start.28
  584.2 255.8 %reduce-scatter.31.cloned.1.call-start = ((), (), s32[]{:S(2)}) async-start(), calls=%async_computation.22 | async-start | bytes 2211840
  586.2 2.0 copy-start.8
  586.2 2.0 copy-start.16
  588.1 2.4 copy-start.34
  588.1 2.4 copy-start.35
  588.1 323.7 %reduce-scatter.29.cloned.1.call-start = ((), (), s32[]{:S(2)}) async-start(), calls=%async_computation.20 | async-start | bytes 2654208 | tf_op jit(solution)/shard_map/reduce_scatter | solution.py:303
  590.5 178.8 %copy-start.17 = (f32[128,768]{1,0:T(8,128)S(1)}, f32[128,768]{1,0:T(8,128)}, u32[]{:S(2)}) copy-start(f32[128,768]{1,0:T(8,128)} %get-tuple-element.320) | copy-start | bytes 1179652
Sparse Core Ops, SparseCore 0:
  62.1 45.7 all-gather.5
  110.5 43.0 all-gather.11
  167.1 21.4 reduce-scatter.14
  191.4 51.9 all-gather.7
  245.7 39.5 all-gather.9
  288.4 22.0 reduce-scatter.16
  328.3 23.6 reduce-scatter.18
  427.3 75.2 reduce-scatter.20
  506.6 74.0 reduce-scatter.22
  584.2 61.6 reduce-scatter.32
  649.6 94.1 reduce-scatter.26
  746.2 23.0 reduce-scatter.24
  773.1 66.8 reduce-scatter.30
  843.9 67.8 reduce-scatter.28
where the time goes:
time: 919 us; the launch traced here: 918 us
  waiting for transfers between devices  598 us (65%)
  blocking collectives  144 us (16%)
  matrix products  101 us (11%)
  other arithmetic  31.8 us (3%)
  local copies, waits for them, and re-layouts  27.6 us (3%)
  between operations  14.5 us (2%)
    reduce_scatter x1, waiting for transfers between devices, local(): lax.psum_scatter(grad_wgu, 'row', scatter_dimension=0, tiled=True)  96.2 us
    reduce_scatter x4, waiting for transfers between devices, column_sum(): lax.psum_scatter(product(left).astype(jnp.bfloat16), 'col', scatter_dimen...  88.2 us
    unnamed x16, waiting for transfers between devices  85.8 us
    reduce_scatter x1, waiting for transfers between devices, local(): lax.psum_scatter(grad_values_all, 'row', scatter_dimension=0, tiled=True)  76.9 us
    reduce_scatter x1, waiting for transfers between devices, local(): lax.psum_scatter(grad_down, 'row', scatter_dimension=1, tiled=True)  69.8 us
    reduce_scatter x1, waiting for transfers between devices, local(): lax.psum_scatter(grad_keys_all, 'row', scatter_dimension=0, tiled=True)  68 us
    all_gather x1, waiting for transfers between devices, local(): lax.all_gather(w_gate_up, 'row', axis=0, tiled=True)  43.2 us
    psum x1, blocking collectives, local(): lax.psum((grad_gain1, grad_bias1, grad_gain2, grad_bias2), ('row', 'col'))  40.1 us
  transfers between devices with their start and end apart: 14, of which 14 were waited for; matrix products, arithmetic and copies ran while one was open for 6% of the time, Pallas kernels for 0%

commit v1 on v0

v1 whole, which is shorter than its diff:
```python
import functools
import math

import jax
import jax.numpy as jnp
from jax import lax
from jax.experimental import pallas as pl
from jax.experimental.pallas import tpu as pltpu
from jax.sharding import PartitionSpec as P

HEAD = 64
ROPE_BASE = 1000.0
NORM_EPS = 1e-12
FAR = -(2.0**100)
LOWEST = -1e30
AUX = 16
BF = jnp.bfloat16
F32 = jnp.float32

CYCLE = (0, 2, 4, 6, 7, 5, 3, 1)
OFFSETS = (0, 2, 1, 3)


def dot(a, b, contract, out=F32):
    return lax.dot_general(a, b, (contract, ((), ())), preferred_element_type=out)


NN = ((1,), (0,))
NT = ((1,), (1,))
TN = ((0,), (0,))


def forward_hop(v):
    n = len(CYCLE)
    return lax.ppermute(v, "row", [(CYCLE[i], CYCLE[(i + 1) % n]) for i in range(n)])


def backward_hop(v):
    n = len(CYCLE)
    return lax.ppermute(v, "row", [(CYCLE[(i + 1) % n], CYCLE[i]) for i in range(n)])


def col_swap(v, mask):
    count = lax.axis_size("col")
    return lax.ppermute(v, "col", [(i, i ^ mask) for i in range(count)])


def cycle_place():
    row = lax.axis_index("row")
    return sum(jnp.where(row == CYCLE[i], i, 0) for i in range(len(CYCLE))).astype(jnp.int32)


def cycle_row(place):
    place = lax.rem(place + 2 * len(CYCLE), len(CYCLE))
    return sum(jnp.where(place == i, CYCLE[i], 0) for i in range(len(CYCLE))).astype(jnp.int32)


def cycle_rounds(block, axis):
    half = block.shape[axis] // 2
    behind, ahead = forward_hop(block), backward_hop(block)
    out = [(behind, ahead)]
    for _ in range(2):
        behind, ahead = forward_hop(behind), backward_hop(ahead)
        out.append((behind, ahead))
    first = forward_hop(lax.slice_in_dim(behind, 0, half, axis=axis))
    second = backward_hop(lax.slice_in_dim(ahead, half, 2 * half, axis=axis))
    return out + [(first, second)]


ROUND_STEPS = (-1, 1, -2, 2, -3, 3, 4, 4)


def cycle_sum(blocks):
    b0, b1, b2, b3, b4a, b4b, b5, b6, b7 = blocks
    half = b4a.shape[0]

    def add(v, block):
        return (v.astype(F32) + block.astype(F32)).astype(BF)

    ahead, back = forward_hop(b4a), backward_hop(b4b)
    ahead = jnp.concatenate([add(ahead, b3[:half]), b3[half:]], axis=0)
    back = jnp.concatenate([b5[:half], add(back, b5[half:])], axis=0)
    for up, down in ((b2, b6), (b1, b7)):
        ahead, back = add(forward_hop(ahead), up), add(backward_hop(back), down)
    ahead, back = forward_hop(ahead), backward_hop(back)
    return b0.astype(F32) + ahead.astype(F32) + back.astype(F32)


def row_sum(blocks):
    if len(blocks) == 1:
        return lax.psum_scatter(blocks[0].astype(F32), "row", scatter_dimension=0, tiled=True)
    return cycle_sum(blocks)


def col_pieces(v):
    side = col_swap(v, 2)
    return [v, side, col_swap(v, 1), col_swap(side, 1)]


def col_exchange(near, far):
    own = near.shape[0] // 2
    other = col_swap(far, 1)
    passed = (near[own:].astype(F32) + other[own:].astype(F32)).astype(BF)
    return near, other, col_swap(passed, 2)


def whole(shape):
    return pl.BlockSpec(shape, lambda *_: (0,) * len(shape))


ANY = pl.BlockSpec(memory_space=pl.ANY)


def call(kernel, name, args, outs, prefetch=(), scratch=(), specs=None, out_specs=None, aliases=None, grid=(1,), flops=0, exps=0):
    args, outs = list(args), list(outs)
    moved = sum(a.size * a.dtype.itemsize for a in args) + sum(
        math.prod(o.shape) * o.dtype.itemsize for o in outs
    )
    return pl.pallas_call(
        kernel,
        grid_spec=pltpu.PrefetchScalarGridSpec(
            num_scalar_prefetch=len(prefetch),
            grid=grid,
            in_specs=specs or [whole(a.shape) for a in args],
            out_specs=out_specs or [whole(o.shape) for o in outs],
            scratch_shapes=list(scratch),
        ),
        out_shape=outs,
        input_output_aliases=aliases or {},
        cost_estimate=pl.CostEstimate(flops=int(flops), bytes_accessed=int(moved), transcendentals=int(exps)),
        name=name,
    )(*prefetch, *args)


def struct(shape, kind):
    return jax.ShapeDtypeStruct(tuple(shape), kind)


def rows_at(start, count):
    return pl.ds(pl.multiple_of(start, 4), count)


def assemble_kernel(split, starts, *refs):
    pieces, (mix, out, held) = refs[:-3], refs[-3:]
    for i, piece in enumerate(pieces):
        held[pl.ds(pl.multiple_of(starts[i], 16), piece.shape[0]), :] = piece[...]
    mix[...] = held[:, :split].T
    out[...] = held[:, split:].T


def assemble(pieces, starts, split):
    width = pieces[0].shape[1]
    total = sum(p.shape[0] for p in pieces)
    return call(
        functools.partial(assemble_kernel, split),
        "assemble",
        pieces,
        [struct((split, total), BF), struct((width - split, total), BF)],
        prefetch=[starts],
        scratch=[pltpu.VMEM((total, width), BF)],
    )


def project_into(pieces, weight, turn, marks, q_out, k_out, v_out, heads):
    half = HEAD // 2
    width = heads * HEAD
    begin = 0
    for piece in pieces:
        count = piece.shape[0]
        lanes = slice(begin, begin + count)
        begin += count
        mixed = dot(weight[...], piece[...], NT)
        cosine, sine = turn[:half, lanes], turn[half:, lanes]
        for h in range(heads):
            for base, out, scale, tail in (
                (0, q_out, 1.0 / math.sqrt(HEAD), AUX),
                (width, k_out, None, 0),
            ):
                at = base + h * HEAD
                first, second = mixed[at : at + half], mixed[at + half : at + HEAD]
                turned = jnp.concatenate(
                    [first * cosine - second * sine, second * cosine + first * sine], axis=0
                )
                if scale is not None:
                    turned = turned * scale
                out[h, :HEAD, lanes] = turned.astype(BF)
                out[h, HEAD:, lanes] = marks[tail : tail + AUX, lanes]
            at = 2 * width + h * HEAD
            v_out[h, :HEAD, lanes] = mixed[at : at + HEAD].astype(BF)
            v_out[h, HEAD:, lanes] = marks[2 * AUX : 3 * AUX, lanes]


def attend_kernel(mode, heads, count, slot, *refs):
    pieces, refs = refs[:count], refs[count:]
    weight, turn, marks = refs[:3]
    refs = refs[3:]
    if mode != "first":
        q_own, top_in, sum_in, acc_in = refs[:4]
        refs = refs[7:]
    if mode == "last":
        w_out, refs = refs[0], refs[1:]
    k, v, q = refs[:3]
    refs = refs[3:]
    project_into(pieces, weight, turn, marks, q, k, v, heads)
    if mode == "first":
        q_own, refs = refs[0], refs[1:]
        q_own[...] = q[...]
    each = range(heads)
    scores = [dot(k[h], q_own[h], TN) for h in each]
    news = [jnp.max(s, axis=0, keepdims=True) for s in scores]
    if mode != "first":
        olds = [top_in[h : h + 1] for h in each]
        news = [jnp.maximum(o, n) for o, n in zip(olds, news)]
        keeps = [jnp.exp(o - n) for o, n in zip(olds, news)]
    weights = [jnp.exp(s - n) for s, n in zip(scores, news)]
    sums = [jnp.sum(w, axis=0, keepdims=True) for w in weights]
    values = [dot(v[h, :HEAD, :], w.astype(BF), NN) for h, w in enumerate(weights)]
    if mode != "first":
        sums = [sum_in[h : h + 1] * keeps[h] + sums[h] for h in each]
        values = [acc_in[h] * keeps[h] + values[h] for h in each]
    if mode != "last":
        top, total, acc = refs
        for h in each:
            top[h : h + 1] = news[h]
            total[h : h + 1] = sums[h]
            acc[h] = values[h]
        return
    near, far, context_bf, context, log_total = refs
    for h in each:
        value = values[h] / sums[h]
        context[h] = value
        context_bf[h * HEAD : (h + 1) * HEAD] = value.astype(BF)
        log_total[h : h + 1] = news[h] + jnp.log(sums[h])
    attn = dot(context_bf[...], w_out[...], TN)
    half = near.shape[0]
    near[...] = attn[:half].astype(BF)
    far[...] = attn[half:].astype(BF)


def attend(mode, pieces, slot, weight, turn, marks, heads, total, group, carried=(), w_out=None):
    width = sum(p.shape[0] for p in pieces)
    rows = HEAD + AUX

    def lanes(*lead):
        return pl.BlockSpec((*lead, width), lambda i, s: (*(0,) * len(lead), s[0]))

    args = [*pieces, weight, turn, marks, *carried]
    specs = [whole(p.shape) for p in pieces]
    specs += [whole(weight.shape), lanes(turn.shape[0]), lanes(marks.shape[0])]
    buffers = [struct((heads, rows, total), BF)] * 3
    outs, out_specs = list(buffers), [lanes(heads, rows)] * 3
    aliases = {}
    if mode != "first":
        specs += [whole(c.shape) for c in carried[:4]] + [ANY] * 3
        base = 1 + len(pieces) + 3 + 4
        aliases = {base: 0, base + 1: 1, base + 2: 2}
    features = weight.shape[1]
    if mode == "last":
        args.append(w_out)
        specs.append(whole(w_out.shape))
        extra = [
            struct((group // 2, features), BF),
            struct((group // 2, features), BF),
            struct((heads * HEAD, group), BF),
            struct((heads, HEAD, group), F32),
            struct((heads, group), F32),
        ]
    else:
        extra = [
            struct((heads, group), F32),
            struct((heads, group), F32),
            struct((heads, HEAD, group), F32),
        ]
        if mode == "first":
            extra = [struct((heads, rows, group), BF)] + extra
    outs += extra
    out_specs += [whole(e.shape) for e in extra]
    scores = heads * width * group
    return call(
        functools.partial(attend_kernel, mode, heads, len(pieces)),
        "attend",
        args,
        outs,
        prefetch=[slot],
        specs=specs,
        out_specs=out_specs,
        aliases=aliases,
        flops=scores * 512,
        exps=scores,
    )


def with_terms(q, g):
    return jnp.concatenate([q[:HEAD], q[HEAD:] + g[HEAD:]], axis=0)


def query_grad_kernel(heads, q, g, k, v, out):
    @pl.when(pl.program_id(0) == 0)
    def _():
        out[...] = jnp.zeros_like(out)

    rows = HEAD + AUX
    each = range(heads)
    terms = [g[h * rows : (h + 1) * rows] for h in each]
    probs = [jnp.exp(dot(k[h], with_terms(q[h], terms[h]), TN)) for h in each]
    grads = [(probs[h] * dot(v[h], terms[h], TN)).astype(BF) for h in each]
    for h in each:
        out[h] += dot(k[h, :HEAD, :], grads[h], NN)


def query_grad(q, g, keys, values, heads, width):
    rows, total = keys.shape[1:]
    group = q.shape[2]
    each = pl.BlockSpec((heads, rows, width), lambda i: (0, 0, i))
    scores = heads * group * total
    return call(
        functools.partial(query_grad_kernel, heads),
        "query_grad",
        [q, g, keys, values],
        [struct((heads, HEAD, group), F32)],
        specs=[whole(q.shape), whole(g.shape), each, each],
        grid=(total // width,),
        flops=scores * 768,
        exps=scores,
    )[0]


def key_grad_kernel(heads, count, carried, slots, *refs):
    pieces, (q, k, v), refs = refs[:count], refs[count : count + 3], refs[count + 3 :]
    rows = HEAD + AUX
    each = range(heads)
    if carried:
        dk_in, dv_in = refs[:2]
        refs = refs[2:]
    dk, dv, norms = refs

    def of(h):
        parts = [p[h * rows : (h + 1) * rows] for p in pieces]
        return parts[0] if count == 1 else jnp.concatenate(parts, axis=1)

    terms = [of(h) for h in each]
    probs = [jnp.exp(dot(with_terms(q[h], terms[h]), k[h], TN)) for h in each]
    grads = [(probs[h] * dot(terms[h], v[h], TN)).astype(BF) for h in each]
    for h in each:
        value = dot(terms[h][:HEAD], probs[h].astype(BF), NN)
        key = dot(q[h, :HEAD, :], grads[h], NN)
        dv[h] = dv_in[h] + value if carried else value
        dk[h] = dk_in[h] + key if carried else key
    for i in range(norms.shape[0]):
        norms[i] = pieces[i][heads * rows : heads * rows + NORM_ROWS, :NORM_LANES].astype(F32)


NORM_LANES = 256


def key_grad(pieces, chunks, slots, q, keys, values, heads, group, sums=()):
    width = sum(p.shape[1] for p in pieces)
    rows = HEAD + AUX
    own = pl.BlockSpec((heads, rows, group), lambda i, s: (0, 0, s[1]))
    specs = [whole(p.shape) for p in pieces]
    specs += [pl.BlockSpec((heads, rows, width), lambda i, s: (0, 0, s[0])), own, own]
    specs += [whole(s.shape) for s in sums]
    scores = heads * group * width
    return call(
        functools.partial(key_grad_kernel, heads, len(pieces), bool(sums)),
        "key_grad",
        [*pieces, q, keys, values, *sums],
        [struct((heads, HEAD, group), F32)] * 2 + [struct((chunks, NORM_ROWS, NORM_LANES), F32)],
        prefetch=[slots],
        specs=specs,
        flops=scores * 1024,
        exps=scores,
    )


def norm_parts(values):
    centered = values - jnp.mean(values, axis=-1, keepdims=True)
    inverse = lax.rsqrt(jnp.mean(centered * centered, axis=-1, keepdims=True) + NORM_EPS)
    return centered * inverse, inverse


def norm_back(grad_out, normed, inverse, gain):
    scaled = grad_out * gain
    grad_in = inverse * (
        scaled
        - jnp.mean(scaled, axis=-1, keepdims=True)
        - normed * jnp.mean(scaled * normed, axis=-1, keepdims=True)
    )
    sums = [jnp.sum(grad_out * normed, axis=0, keepdims=True), jnp.sum(grad_out, axis=0, keepdims=True)]
    return grad_in, sums


def col_total(near, other, last):
    own = last.shape[0]
    return near[:own].astype(F32) + other[:own].astype(F32) + last[...].astype(F32)


def first_norm_kernel(near, other, last, tokens, gain, bias, residual, hidden):
    value = tokens[...].astype(F32) + col_total(near, other, last)
    residual[...] = value
    normed, _ = norm_parts(value)
    hidden[...] = (normed * gain[...] + bias[...]).astype(BF)


def second_norm_kernel(near, other, last, residual, gain1, bias1, gain2, bias2, cotangent, result, grad, grad_bf, sums):
    hidden = norm_parts(residual[...])[0] * gain1[...] + bias1[...]
    normed, inverse = norm_parts(hidden + col_total(near, other, last))
    result[...] = (normed * gain2[...] + bias2[...]).astype(BF)
    value, (dgain, dbias) = norm_back(cotangent[...].astype(F32), normed, inverse, gain2[...])
    grad[...] = value
    grad_bf[...] = value.astype(BF)
    sums[0:1] = dgain
    sums[1:2] = dbias


def first_norm_back_kernel(near, other, last, residual, gain, grad2, sums2, grad, package):
    normed, inverse = norm_parts(residual[...])
    grad_out = grad2[...] + col_total(near, other, last)
    value, (dgain, dbias) = norm_back(grad_out, normed, inverse, gain[...])
    grad[...] = value
    own = value.shape[0]
    package[:own] = value.astype(BF)
    sums = jnp.concatenate([dgain, dbias, sums2[0:1], sums2[1:2]], axis=0)
    high = sums.astype(BF)
    low = (sums - high.astype(F32)).astype(BF)
    blank = jnp.zeros((8, sums.shape[1]), F32)
    package[own:] = jnp.concatenate([high.astype(F32), low.astype(F32), blank], axis=0).astype(BF)


def stacked(refs, rows):
    return jnp.concatenate([r[:rows] for r in refs], axis=0)


def forward_kernel(count, units, starts, *refs):
    pieces, hidden, (gu, dn, gate_up, inner, near, far) = refs[:count], refs[count:-6], refs[-6:]
    for i, piece in enumerate(pieces):
        rows = pl.ds(pl.multiple_of(starts[i], 16), piece.shape[0])
        gu[rows, :] = piece[:, : 2 * units]
        dn[rows, :] = piece[:, 2 * units :]
    pairs = len(hidden) // 2
    for out, part in ((near, hidden[:pairs]), (far, hidden[pairs:])):
        x = stacked(part, part[0].shape[0])
        size = x.shape[0]
        begin = 0 if out is near else size
        both = dot(x, gu[...], NN)
        gate_up[begin : begin + size] = both
        up, gate = both[:, :units], both[:, units:]
        value = (gate * jax.nn.sigmoid(gate) * up).astype(BF)
        inner[begin : begin + size] = value
        out[...] = dot(value, dn[...], NT).astype(BF)


def backward_kernel(units, *refs):
    pieces, (gu, dn, gate_up, grads, near, far) = refs[:-6], refs[-6:]
    pairs = len(pieces) // 2
    for out, part in ((near, pieces[:pairs]), (far, pieces[pairs:])):
        g = stacked(part, part[0].shape[0])
        size = g.shape[0]
        begin = 0 if out is near else size
        grad_inner = dot(g, dn[...], NN)
        up = gate_up[begin : begin + size, :units]
        gate = gate_up[begin : begin + size, units:]
        sigma = jax.nn.sigmoid(gate)
        grads[begin : begin + size, :units] = (grad_inner * gate * sigma).astype(BF)
        grads[begin : begin + size, units:] = (
            grad_inner * up * sigma * (1.0 + gate * (1.0 - sigma))
        ).astype(BF)
        out[...] = dot(grads[begin : begin + size], gu[...], NT).astype(BF)


def write_blocks(held, starts, outs):
    for i, out in enumerate(outs):
        out[...] = held[pl.ds(pl.multiple_of(starts[i], 16), out.shape[0]), :]


def block_structs(features, width, ring):
    if not ring:
        return [struct((features, width), BF)]
    share = features // len(CYCLE)
    sizes = [share] * 4 + [share // 2] * 2 + [share] * 3
    return [struct((n, width), BF) for n in sizes]


def ffn_grad_kernel(units, n_blocks, starts, *refs):
    hidden, g, (grads, inner) = refs[:4], refs[4:8], refs[8:10]
    outs, held = refs[10 : 10 + n_blocks], refs[10 + n_blocks]
    own = hidden[0].shape[0]
    turned = stacked(hidden, own).T
    for t in range(0, 2 * units, units):
        held[:, t : t + units] = dot(turned, grads[:, t : t + units], NN).astype(BF)
    held[:, 2 * units :] = dot(stacked(g, own).T, inner[...], NN).astype(BF)
    write_blocks(held, starts, outs)


def prepare_kernel(heads, own, *refs):
    pieces, (w_out, context, log_total, package) = refs[:4], refs[4:]
    g = stacked(pieces, own)
    rows = HEAD + AUX
    grad = dot(w_out[...], g, NT).astype(BF)
    index = lax.broadcasted_iota(jnp.int32, (AUX, g.shape[0]), 0)
    for h in range(heads):
        part = grad[h * HEAD : (h + 1) * HEAD]
        package[h * rows : h * rows + HEAD] = part
        delta = jnp.sum(part.astype(F32) * context[h], axis=0, keepdims=True)
        tail = jnp.zeros(index.shape, F32)
        for at, value in ((8, -log_total[h : h + 1]), (11, -delta)):
            for j in range(3):
                high = value.astype(BF).astype(F32)
                tail = jnp.where(index == at + j, high, tail)
                value = value - high
        package[h * rows + HEAD : (h + 1) * rows] = tail.astype(BF)

    def sums(piece):
        both = piece[own : own + 16].astype(F32)
        return both[:4] + both[4:8]

    total = (sums(pieces[0]) + sums(pieces[1])) + (sums(pieces[2]) + sums(pieces[3]))
    high = total.astype(BF).astype(F32)
    both = jnp.concatenate([high, total - high], axis=0)
    base = heads * rows
    package[base:, NORM_LANES:] = jnp.zeros((package.shape[0] - base, package.shape[1] - NORM_LANES), BF)
    parts = [both[:, i * NORM_LANES : (i + 1) * NORM_LANES] for i in range(both.shape[1] // NORM_LANES)]
    parts.append(jnp.zeros((package.shape[0] - base - 8 * len(parts), NORM_LANES), F32))
    package[base:, :NORM_LANES] = jnp.concatenate(parts, axis=0).astype(BF)


def turn_back(first, second, cosine, sine):
    return jnp.concatenate([first * cosine + second * sine, second * cosine - first * sine], axis=0)


def early_grad_kernel(heads, own, n_x, n_blocks, slots, starts, *refs):
    x_refs, g_refs, refs = refs[:n_x], refs[n_x : n_x + 4], refs[n_x + 4 :]
    grad_query, turn, context, mixed, *refs = refs
    outs, held = refs[:n_blocks], refs[n_blocks]
    half = HEAD // 2
    scale = 1.0 / math.sqrt(HEAD)
    for h in range(heads):
        value = grad_query[h] * scale
        mixed[h * HEAD : (h + 1) * HEAD] = turn_back(value[:half], value[half:], turn[:half], turn[half:]).astype(BF)
    x = stacked(x_refs, x_refs[0].shape[0])
    width = heads * HEAD
    held[:, :width] = dot(mixed[...], x, NN).T.astype(BF)
    held[:, width:] = dot(context[...], stacked(g_refs, own), NN).T.astype(BF)
    write_blocks(held, starts, outs)


def late_grad_kernel(heads, n_x, n_blocks, slots, starts, *refs):
    x_refs, refs = refs[:n_x], refs[n_x:]
    mixed_q, grad_key, grad_value, turn, weight, near, far, *refs = refs
    outs, held, mixed = refs[:n_blocks], refs[n_blocks], refs[n_blocks + 1]
    half = HEAD // 2
    width = heads * HEAD
    mixed[:width] = mixed_q[...]
    for h in range(heads):
        value = grad_key[h]
        mixed[width + h * HEAD : width + (h + 1) * HEAD] = turn_back(
            value[:half], value[half:], turn[:half], turn[half:]
        ).astype(BF)
        mixed[2 * width + h * HEAD : 2 * width + (h + 1) * HEAD] = grad_value[h].astype(BF)
    back = dot(mixed[...], weight[...], TN)
    size = near.shape[0]
    near[...] = back[:size].astype(BF)
    far[...] = back[size:].astype(BF)
    x = stacked(x_refs, x_refs[0].shape[0])
    held[...] = dot(mixed[width:], x, NN).T.astype(BF)
    write_blocks(held, starts, outs)


NORM_ROWS = 24


def norm_total_kernel(rows, *refs):
    pieces, (out, held) = refs[:-2], refs[-2:]
    at = 0
    for piece in pieces:
        for i in range(piece.shape[0]):
            held[rows[at]] = piece[i]
            at += 1
    total = held[0]
    for r in range(1, at):
        total = total + held[r]
    for i in range(NORM_ROWS // 8):
        part = total[8 * i : 8 * i + 8]
        out[:, i * NORM_LANES : (i + 1) * NORM_LANES] = part[:4] + part[4:]


def slot_tables(seq_lengths, packed_order, chunk_rows, col, local):
    cols = lax.axis_size("col")
    blocks = packed_order.reshape(-1, local)
    wanted = (chunk_rows[:, None] * cols + jnp.stack([col ^ o for o in OFFSETS])[None, :]).reshape(-1)
    index = jnp.arange(blocks.shape[0], dtype=jnp.int32)
    slots = jnp.sum(
        jnp.where(wanted[:, None, None] == index[None, :, None], blocks[None], 0), axis=1
    ).reshape(1, -1)
    count = seq_lengths.shape[0]
    seq = jnp.zeros_like(slots)
    start = jnp.zeros_like(slots)
    end = jnp.int32(0)
    for s in range(count):
        end = end + seq_lengths[s]
        passed = slots >= end
        seq = seq + passed.astype(jnp.int32)
        start = jnp.where(passed, end, start)
    positions = (slots - start).astype(F32)
    half = HEAD // 2
    freqs = ROPE_BASE ** (-jnp.arange(half, dtype=F32) * 2.0 / HEAD)
    angles = positions * freqs[:, None]
    turn = jnp.concatenate([jnp.cos(angles), jnp.sin(angles)], axis=0)
    line = jnp.arange(3 * AUX, dtype=jnp.int32)[:, None]
    member = lax.rem(line, AUX) == seq
    ones = ((line >= 8) & (line < 11)) | ((line >= 2 * AUX + 11) & (line < 2 * AUX + 14))
    marks = jnp.where(ones, 1.0, 0.0)
    marks = jnp.where((line < 8) & member, 1.0, marks)
    marks = jnp.where((line >= AUX) & (line < AUX + 8) & ~member, FAR, marks)
    return turn, marks.astype(BF)


def local(
    tokens,
    w_qkv,
    w_out,
    w_gate_up,
    w_down,
    gain1,
    bias1,
    gain2,
    bias2,
    cotangent,
    seq_lengths,
    packed_order,
):
    rows = lax.axis_size("row")
    row, col = lax.axis_index("row"), lax.axis_index("col")
    ring = rows == len(CYCLE)
    own, features = tokens.shape
    group = own * lax.axis_size("col")
    total = group * rows
    share = w_qkv.shape[0]
    width = w_qkv.shape[2]
    heads = width // HEAD
    units = w_gate_up.shape[2]
    gains = [v.reshape(1, features) for v in (gain1, bias1, gain2, bias2)]

    early = jnp.concatenate([w_qkv.reshape(share, 3 * width), w_out.T], axis=1)
    late = jnp.concatenate([w_gate_up.reshape(share, 2 * units), w_down.T], axis=1)

    pair = jnp.concatenate([tokens, col_swap(tokens, 2)], axis=0)
    x_pieces = [pair, col_swap(pair, 1)]
    if ring:
        place = cycle_place()
        steps = [cycle_row(place + s) for s in ROUND_STEPS]
        half = share // 2
        starts = jnp.stack(
            [row * share] + [r * share for r in steps[:7]] + [steps[7] * share + half]
        )
        ahead = [cycle_row(place + s) * share for s in range(8)]
        block_starts = jnp.stack(ahead[:5] + [ahead[4] + half] + ahead[5:])
        chunk_rows = jnp.stack(steps[:6] + [row, steps[6]])
        rounds = cycle_rounds(early, 0)
        w_mix, full_out = assemble([early] + [p for r in rounds for p in r], starts, 3 * width)
    else:
        starts = block_starts = jnp.zeros((1,), jnp.int32)
        chunk_rows = jnp.arange(rows, dtype=jnp.int32)
        early_full = lax.all_gather(early, "row", axis=0, tiled=True)
        w_mix, full_out = assemble([early_full], starts, 3 * width)

    turn, marks = slot_tables(seq_lengths, packed_order, chunk_rows, col, own)
    fixed = (w_mix, turn, marks, heads, total, group)

    def at(slot):
        return jnp.asarray(slot, jnp.int32).reshape(1)

    own_slot = at(6) if ring else at(row)
    keys, values, queries, own_q, *state = attend("first", x_pieces, own_slot, *fixed)
    if ring:
        rounds = cycle_rounds(pair, 0)
        for i, pieces in enumerate(rounds[:3]):
            pieces = [q for p in pieces for q in (p, col_swap(p, 1))]
            keys, values, queries, *state = attend(
                "middle", pieces, at(i), *fixed, (own_q, *state, keys, values, queries)
            )
        pieces = [*rounds[3], *(col_swap(p, 1) for p in rounds[3])]
        keys, values, queries, *finished = attend(
            "last", pieces, at(7), *fixed, (own_q, *state, keys, values, queries), full_out
        )
    else:
        blocks = lax.all_gather(jnp.concatenate(x_pieces, axis=0), "row", axis=0, tiled=False)

        def block(i):
            slot = lax.rem(row + i, rows)
            return [lax.dynamic_index_in_dim(blocks, slot, 0, keepdims=False)], at(slot)

        def step(i, carried):
            *state, keys, values, queries = carried
            keys, values, queries, *state = attend(
                "middle", *block(i), *fixed, (own_q, *state, keys, values, queries)
            )
            return (*state, keys, values, queries)

        *state, keys, values, queries = lax.fori_loop(1, rows - 1, step, (*state, keys, values, queries))
        keys, values, queries, *finished = attend(
            "last", *block(rows - 1), *fixed, (own_q, *state, keys, values, queries), full_out
        )
    near, far, context_bf, context, log_total = finished

    if ring:
        late, _ = lax.optimization_barrier((late, rounds[1]))
        late_pieces = [late] + [p for r in cycle_rounds(late, 0) for p in r]
    else:
        late_pieces = [lax.all_gather(late, "row", axis=0, tiled=True)]

    part = struct((group // 2, features), BF)
    flat = struct((own, features), F32)
    residual1, hidden = call(
        first_norm_kernel,
        "first_norm",
        [*col_exchange(near, far), tokens, *gains[:2]],
        [flat, struct((own, features), BF)],
    )
    hidden_pieces = col_pieces(hidden)
    w_gu, w_dn, gate_up, inner, near, far = call(
        functools.partial(forward_kernel, len(late_pieces), units),
        "ffn_forward",
        [*late_pieces, *hidden_pieces],
        [
            struct((features, 2 * units), BF),
            struct((features, units), BF),
            struct((group, 2 * units), F32),
            struct((group, units), BF),
            part,
            part,
        ],
        prefetch=[starts],
        flops=6 * group * features * units,
    )
    result, grad_res2, grad_bf, sums2 = call(
        second_norm_kernel,
        "second_norm",
        [*col_exchange(near, far), residual1, *gains, cotangent],
        [struct((own, features), BF), flat, struct((own, features), BF), struct((8, features), F32)],
    )
    grad_pieces = col_pieces(grad_bf)
    grad_gate_up, near, far = call(
        functools.partial(backward_kernel, units),
        "ffn_backward",
        [*grad_pieces, w_gu, w_dn, gate_up],
        [struct((group, 2 * units), BF), part, part],
        flops=6 * group * features * units,
    )
    exchanged = col_exchange(near, far)
    outs = block_structs(features, 3 * units, ring)
    blocks = call(
        functools.partial(ffn_grad_kernel, units, len(outs)),
        "ffn_grad",
        [*hidden_pieces, *grad_pieces, grad_gate_up, inner],
        outs,
        prefetch=[block_starts],
        scratch=[pltpu.VMEM((features, 3 * units), BF)],
        flops=6 * group * features * units,
    )
    ffn_grad = row_sum(blocks)
    grad_res1, package = call(
        first_norm_back_kernel,
        "first_norm_back",
        [*exchanged, residual1, gains[0], grad_res2, sums2],
        [flat, struct((own + 16, features), BF)],
    )
    attn_pieces = col_pieces(package)
    (package,) = call(
        functools.partial(prepare_kernel, heads, own),
        "prepare",
        [*attn_pieces, full_out, context, log_total],
        [struct((heads * (HEAD + AUX) + 32, group), BF)],
        flops=2 * width * features * group,
    )
    grad_query = query_grad(own_q, package, keys, values, heads, min(2 * group, total))
    own_turn = pl.BlockSpec((HEAD, group), lambda i, s, b: (0, s[0]))
    outs = block_structs(features, 2 * width, ring)
    args = [*x_pieces, *attn_pieces, grad_query, turn, context_bf]
    specs = [whole(a.shape) for a in args]
    specs[-2] = own_turn
    mixed_q, *blocks = call(
        functools.partial(early_grad_kernel, heads, own, len(x_pieces), len(outs)),
        "early_grad",
        args,
        [struct((width, group), BF), *outs],
        prefetch=[own_slot, block_starts],
        scratch=[pltpu.VMEM((features, 2 * width), BF)],
        specs=specs,
        flops=4 * width * features * group,
    )
    early_grad = row_sum(blocks)

    def key_step(pieces, chunks, slot, sums):
        slots = jnp.concatenate([at(slot), own_slot])
        *sums, norms = key_grad(pieces, chunks, slots, queries, keys, values, heads, group, tuple(sums))
        return sums, norms

    norm_out = struct((4, features), F32)
    if ring:
        rounds = cycle_rounds(package, 1)
        sums, norms = key_step([package], 1, 6, ())
        norm_pieces = [norms]
        for i, pieces in enumerate(rounds[:3]):
            sums, norms = key_step(pieces, 2, i, sums)
            norm_pieces.append(norms)
        sums, norms = key_step(rounds[3], 1, 7, sums)
        norm_pieces.append(norms)
        (norm_sums,) = call(
            norm_total_kernel,
            "norm_total",
            norm_pieces,
            [norm_out],
            prefetch=[jnp.stack([row] + steps[:7])],
            scratch=[pltpu.VMEM((rows, NORM_ROWS, NORM_LANES), F32)],
        )
    else:
        packages = lax.all_gather(package, "row", axis=0, tiled=False)

        def step(i, carried):
            sums, norms = carried
            piece = lax.dynamic_index_in_dim(packages, i, 0, keepdims=False)
            sums, more = key_step([piece], 1, i, sums)
            return tuple(sums), norms + more

        zeros = jnp.zeros((heads, HEAD, group), F32)
        sums, norms = lax.fori_loop(
            0, rows, step, ((zeros, zeros), jnp.zeros((1, NORM_ROWS, NORM_LANES), F32))
        )
        (norm_sums,) = call(
            norm_total_kernel,
            "norm_total",
            [norms],
            [norm_out],
            prefetch=[jnp.zeros((1,), jnp.int32)],
            scratch=[pltpu.VMEM((1, NORM_ROWS, NORM_LANES), F32)],
        )
    args = [*x_pieces, mixed_q, *sums, turn, w_mix]
    specs = [whole(a.shape) for a in args]
    specs[-2] = own_turn
    near, far, *blocks = call(
        functools.partial(late_grad_kernel, heads, len(x_pieces), len(outs)),
        "late_grad",
        args,
        [part, part, *outs],
        prefetch=[own_slot, block_starts],
        scratch=[pltpu.VMEM((features, 2 * width), BF), pltpu.VMEM((3 * width, group), BF)],
        specs=specs,
        flops=10 * width * features * group,
    )
    late_grad = row_sum(blocks)
    near, other, last = col_exchange(near, far)
    grad_tokens = grad_res1 + (
        near[:own].astype(F32) + other[:own].astype(F32) + last.astype(F32)
    )
    grad_mix = jnp.concatenate([early_grad[:, :width], late_grad], axis=1)
    return (
        result,
        grad_tokens,
        grad_mix.reshape(share, 3, width),
        early_grad[:, width:].T,
        ffn_grad[:, : 2 * units].reshape(share, 2, units),
        ffn_grad[:, 2 * units :].T,
        norm_sums[0],
        norm_sums[1],
        norm_sums[2],
        norm_sums[3],
    )


def solution(mesh):
    placed = (
        P(("row", "col"), None),
        P("row", None, "col"),
        P("col", "row"),
        P("row", None, "col"),
        P("col", "row"),
        P(),
        P(),
        P(),
        P(),
        P(("row", "col"), None),
        P(),
        P(),
    )
    return jax.shard_map(
        local,
        mesh=mesh,
        in_specs=placed,
        out_specs=(
            P(("row", "col"), None),
            P(("row", "col"), None),
            P("row", None, "col"),
            P("col", "row"),
            P("row", None, "col"),
            P("col", "row"),
            P(),
            P(),
            P(),
            P(),
        ),
        check_vma=False,
    )
```

time: 919 us -> 334 us (0.36)
  waiting for transfers between devices: 598 us -> 98.2 us
  blocking collectives: 144 us -> 0 us
  Pallas kernels: 0 us -> 112 us
  matrix products: 101 us -> 0 us
  starting transfers between devices: 0.8 us -> 67.1 us
  other arithmetic: 31.8 us -> 18.1 us
  between operations: 14.5 us -> 4.17 us
    reduce_scatter x8 -> x0, waiting for transfers between devices: 399 us -> none  [the longest x1 96.2 us: local(): lax.psum_scatter(grad_wgu, 'row', scatter_dimension=0, tiled=True)]
    all_gather x4 -> x0, waiting for transfers between devices: 113 us -> none  [the longest x1 43.2 us: local(): lax.all_gather(w_gate_up, 'row', axis=0, tiled=True)]
    pallas_call x0 -> x22, Pallas kernels: none -> 112 us  [call(): pl.pallas_call(kernel, grid_spec=pltpu.PrefetchScalarGridSpec(num_scalar_...]
    all_gather x6 -> x0, blocking collectives: 104 us -> none  [the longest x1 38.8 us: local(): lax.all_gather(w_qkv, 'row', axis=0, tiled=True)]
    dot_general x22 -> x0, matrix products: 99.4 us -> none  [the longest x3 25.2 us: score_block(): jnp.einsum('qhd,khd->hqk', queries, key_rows.reshape(count, heads, head),...]
    ppermute x0 -> x83, waiting for transfers between devices: none -> 98.2 us  [the longest x28 47.7 us: forward_hop(): lax.ppermute(v, 'row', [(CYCLE[i], CYCLE[(i + 1) % n]) for i in range(n)])]
    unnamed x16 -> x0, waiting for transfers between devices: 85.8 us -> none
    ppermute x0 -> x83, starting transfers between devices: none -> 67.1 us  [the longest x28 39.5 us: forward_hop(): lax.ppermute(v, 'row', [(CYCLE[i], CYCLE[(i + 1) % n]) for i in range(n)])]
  transfers between devices with their start and end apart: 14 -> 83, of which waited for: 14 -> 33; matrix products, arithmetic and copies ran while one was open for 6% -> 10% of each run, Pallas kernels for 0% -> 24%
where the time goes in v1:
time: 334 us; the launch traced here: 328 us
  Pallas kernels  112 us (34%)
  waiting for transfers between devices  98.2 us (29%)
  starting transfers between devices  67.1 us (20%)
  local copies, waits for them, and re-layouts  28 us (8%)
  other arithmetic  18.1 us (5%)
  between operations  4.17 us (1%)
    pallas_call x22, Pallas kernels, call(): pl.pallas_call(kernel, grid_spec=pltpu.PrefetchScalarGridSpec(num_scalar_...  112 us
    ppermute x28, waiting for transfers between devices, forward_hop(): lax.ppermute(v, 'row', [(CYCLE[i], CYCLE[(i + 1) % n]) for i in range(n)])  47.7 us
    ppermute x28, starting transfers between devices, forward_hop(): lax.ppermute(v, 'row', [(CYCLE[i], CYCLE[(i + 1) % n]) for i in range(n)])  39.5 us
    ppermute x27, waiting for transfers between devices, col_swap(): return lax.ppermute(v, 'col', [(i, i ^ mask) for i in range(count)])  33.2 us
    ppermute x28, starting transfers between devices, backward_hop(): lax.ppermute(v, 'row', [(CYCLE[(i + 1) % n], CYCLE[i]) for i in range(n)])  18.6 us
    ppermute x28, waiting for transfers between devices, backward_hop(): lax.ppermute(v, 'row', [(CYCLE[(i + 1) % n], CYCLE[i]) for i in range(n)])  17.3 us
    unnamed x162, local copies, waits for them, and re-layouts  13 us
    ppermute x27, starting transfers between devices, col_swap(): return lax.ppermute(v, 'col', [(i, i ^ mask) for i in range(count)])  9.03 us
  transfers between devices with their start and end apart: 83, of which 33 were waited for; matrix products, arithmetic and copies ran while one was open for 10% of the time, Pallas kernels for 24%

profile of v1, /device:TPU:0, one launch (start us, length us, event | category | flops | bytes accessed | tf_op | source)
XLA Modules:
  0.0 327.8 jit_solution(6455674932119896689)
XLA Ops:
  3.0 3.1 collective-permute-start.19
  6.0 2.0 collective-permute-start
  11.1 1.5 collective-permute-done
  12.6 1.8 collective-permute-start.1
  17.6 4.9 %collective-permute-done.1.refs_0_ = bf16[256,768]{1,0:T(8,128)(2,1)S(1)} collective-permute-done((bf16[256,768]{1,0:T(8,128)(2,1)S(1)}, bf16[256,768]{1,0:T(8,128)(2,1)S(1)}, u32[]{:S(2)}, u32[]{:S(2)}) %collective-permute-start.1) | collective-permute-done | bytes 393248 | tf_op jit(solution)/shard_map/ppermute | solution.py:35
  24.5 1.9 multiply_cosine_fusion
  26.4 1.5 collective-permute-start.21
  28.5 5.5 %collective-permute-done.2.refs_0_ = bf16[256,768]{1,0:T(8,128)(2,1)S(1)} collective-permute-done((bf16[256,768]{1,0:T(8,128)(2,1)S(1)}, bf16[256,768]{1,0:T(8,128)(2,1)S(1)}, u32[]{:S(2)}, u32[]{:S(2)}) %collective-permute-start.2) | collective-permute-done | bytes 393248 | tf_op jit(solution)/shard_map/ppermute | solution.py:35
  39.3 7.2 %collective-permute-done.23.refs_5_ = bf16[96,768]{1,0:T(8,128)(2,1)S(1)} collective-permute-done((bf16[96,768]{1,0:T(8,128)(2,1)S(1)}, bf16[96,768]{1,0:T(8,128)(2,1)S(1)}, u32[]{:S(2)}, u32[]{:S(2)}) %collective-permute-start.23) | collective-permute-done | bytes 147488 | tf_op jit(solution)/shard_map/ppermute | solution.py:35
  48.6 2.2 collective-permute-done.25.refs_7_
  51.8 1.6 collective-permute-start.5
  57.0 1.6 collective-permute-start.14
  59.2 5.6 %collective-permute-done.5.refs_1_ = bf16[96,2304]{1,0:T(8,128)(2,1)S(1)} collective-permute-done((bf16[96,2304]{1,0:T(8,128)(2,1)S(1)}, bf16[96,2304]{1,0:T(8,128)(2,1)S(1)}, u32[]{:S(2)}, u32[]{:S(2)}) %collective-permute-start.5) | collective-permute-done | bytes 442400 | tf_op jit(solution)/shard_map/ppermute | solution.py:35
  67.3 3.5 %assemble.1 = (bf16[576,768]{1,0:T(8,128)(2,1)}, bf16[192,768]{1,0:T(8,128)(2,1)}) custom-call(s32[9]{0:T(128)} %stack.112.starts, bf16[96,768]{1,0:T(8,128)(2,1)} %copy-done.13, bf16[96,768]{1,0:T(8,128)(2,1)} %collective-permute-done.19.refs_1_, bf16[96,768]{1,0:T(8,128)(2,1)} %collective-permute-done.20.refs_2_, bf16[96,768]{1,0:T(8,128)(2,1)} %copy-done.47, ...), custom_call_target="tpu_custom_call" | custom-call | bytes 2359296 | tf_op jit(solution)/shard_map/assemble/pallas_call | solution.py:119
  70.8 4.1 %attend.5 = (bf16[3,80,4096]{2,1,0:T(8,128)(2,1)}, bf16[3,80,4096]{2,1,0:T(8,128)(2,1)}, bf16[3,80,4096]{2,1,0:T(8,128)(2,1)}, bf16[3,80,512]{2,1,0:T(8,128)(2,1...) custom-call(s32[1]{0:T(128)} %constant.115.clone.1.slot.slots, bf16[256,768]{1,0:T(8,128)(2,1)} %copy-done, ...), custom_call_target="tpu_custom_call" | custom-call | flops 402653184 | bytes 9662464 | tf_op jit(solution)/shard_map/attend/pallas_call | solution.py:119
  75.6 6.2 %attend.6 = (bf16[3,80,4096]{2,1,0:T(8,128)(2,1)}, bf16[3,80,4096]{2,1,0:T(8,128)(2,1)}, bf16[3,80,4096]{2,1,0:T(8,128)(2,1)}, f32[3,512]{1,0:T(4,128)}, f32[3,512]{1,0:T(4,128)}, /*index=5*/f32[3,64,512]{2,1,0:T(8,128)}) custom-call(s32[1]{0:T(128)} %constant.118.clone.1.slot, ...), custom_call_target="tpu_custom_call", output_to_operand_aliasing={{0}: (12, {}), {1}: (13, {}), {2}: (14, {})} | custom-call | flops 805306368 | bytes 16752640 | tf_op jit(solution)/shard_map/attend/pallas_call | solution.py:119
  81.7 6.2 %attend.7 = (bf16[3,80,4096]{2,1,0:T(8,128)(2,1)}, bf16[3,80,4096]{2,1,0:T(8,128)(2,1)}, bf16[3,80,4096]{2,1,0:T(8,128)(2,1)}, f32[3,512]{1,0:T(4,128)}, f32[3,512]{1,0:T(4,128)}, /*index=5*/f32[3,64,512]{2,1,0:T(8,128)}) custom-call(s32[1]{0:T(128)} %constant.117.clone.1.slot, ...), custom_call_target="tpu_custom_call", output_to_operand_aliasing={{0}: (12, {}), {1}: (13, {}), {2}: (14, {})} | custom-call | flops 805306368 | bytes 16752640 | tf_op jit(solution)/shard_map/attend/pallas_call | solution.py:119
  87.9 1.6 collective-permute-start.7
  91.0 6.2 %attend.8 = (bf16[3,80,4096]{2,1,0:T(8,128)(2,1)}, bf16[3,80,4096]{2,1,0:T(8,128)(2,1)}, bf16[3,80,4096]{2,1,0:T(8,128)(2,1)}, f32[3,512]{1,0:T(4,128)}, f32[3,512]{1,0:T(4,128)}, /*index=5*/f32[3,64,512]{2,1,0:T(8,128)}) custom-call(s32[1]{0:T(128)} %constant.116.clone.1.slot, ...), custom_call_target="tpu_custom_call", output_to_operand_aliasing={{0}: (12, {}), {1}: (13, {}), {2}: (14, {})} | custom-call | flops 805306368 | bytes 16752640 | tf_op jit(solution)/shard_map/attend/pallas_call | solution.py:119
  98.0 6.0 %attend.9 = (bf16[3,80,4096]{2,1,0:T(8,128)(2,1)}, bf16[3,80,4096]{2,1,0:T(8,128)(2,1)}, bf16[3,80,4096]{2,1,0:T(8,128)(2,1)}, bf16[256,768]{1,0:T(8,128)(2,1)},...) custom-call(s32[1]{0:T(128)} %constant.102.clone.1.slot, ...), custom_call_target="tpu_custom_call", output_to_operand_aliasing={{0}: (12, {}), {1}: (13, {}), {2}: (14, {})} | custom-call | flops 402653184 | bytes 17238016 | tf_op jit(solution)/shard_map/attend/pallas_call | solution.py:119
  104.0 1.6 collective-permute-start.9
  107.2 1.6 collective-permute-start.35
  110.0 4.1 %collective-permute-done.35.last = bf16[128,768]{1,0:T(8,128)(2,1)S(1)} collective-permute-done((bf16[128,768]{1,0:T(8,128)(2,1)S(1)}, bf16[128,768]{1,0:T(8,128)(2,1)S(1)}, u32[]{:S(2)}, u32[]{:S(2)}) %collective-permute-start.35) | collective-permute-done | bytes 196640 | tf_op jit(solution)/shard_map/ppermute | solution.py:45
  114.7 2.2 first_norm.1
  116.9 1.5 collective-permute-start.36
  118.5 1.6 collective-permute-start.11
  121.1 1.9 collective-permute-done.36.refs_10_.refs_1_
  123.1 1.6 collective-permute-done.11.refs_7_
  124.7 1.9 collective-permute-done.12.refs_8_
  128.1 6.9 %ffn_forward.1 = (bf16[768,1536]{1,0:T(8,128)(2,1)}, bf16[768,768]{1,0:T(8,128)(2,1)}, f32[512,1536]{1,0:T(8,128)}, bf16[512,768]{1,0:T(8,128)(2,1)}, bf16[256,7...) custom-call(s32[9]{0:T(128)} %stack.112.starts, bf16[96,2304]{1,0:T(8,128)(2,1)} %copy-done.14, bf16[96,2304]{1,0:T(8,128)(2,1)} %copy-done.68, ...), custom_call_target="tpu_custom_call" | custom-call | flops 1811939328 | bytes 12582912 | tf_op jit(solution)/shard_map/ffn_forward/pallas_call | solution.py:119
  135.0 1.9 collective-permute-done.39.other
  139.8 5.3 %collective-permute-done.40.last = bf16[128,768]{1,0:T(8,128)(2,1)S(1)} collective-permute-done((bf16[128,768]{1,0:T(8,128)(2,1)S(1)}, bf16[128,768]{1,0:T(8,128)(2,1)S(1)}, u32[]{:S(2)}, u32[]{:S(2)}) %collective-permute-start.40) | collective-permute-done | bytes 196640 | tf_op jit(solution)/shard_map/ppermute | solution.py:45
  145.8 2.8 second_norm.1
  149.1 5.8 %collective-permute-done.41.refs_1_.refs_5_ = bf16[128,768]{1,0:T(8,128)(2,1)S(1)} collective-permute-done((bf16[128,768]{1,0:T(8,128)(2,1)}, bf16[128,768]{1,0:T(8,128)(2,1)S(1)}, u32[]{:S(2)}, u32[]{:S(2)}) %collective-permute-start.41) | collective-permute-done | bytes 196640 | tf_op jit(solution)/shard_map/ppermute | solution.py:45
  157.0 6.5 %ffn_backward.1 = (bf16[512,1536]{1,0:T(8,128)(2,1)}, bf16[256,768]{1,0:T(8,128)(2,1)}, bf16[256,768]{1,0:T(8,128)(2,1)}) custom-call(bf16[128,768]{1,0:T(8,128)(2,1)} %get-tuple-element.143.refs_0_.refs_4_, bf16[128,768]{1,0:T(8,128)(2,1)} %copy-done.39, bf16[128,768]{1,0:T(8,128)(2,1)} %copy-done.40, bf16[128,768]{1,0:T(8,128)(2,1)} %copy-done.41, ...), custom_call_target="tpu_custom_call" | custom-call | flops 1811939328 | bytes 9830400 | tf_op jit(solution)/shard_map/ffn_backward/pallas_call | solution.py:119
  163.5 6.9 %ffn_grad.1 = (bf16[96,2304]{1,0:T(8,128)(2,1)}, bf16[96,2304]{1,0:T(8,128)(2,1)}, bf16[96,2304]{1,0:T(8,128)(2,1)}, bf16[96,2304]{1,0:T(8,128)(2,1)}, bf16[48,2...) custom-call(s32[9]{0:T(128)} %stack.131.starts, ...), custom_call_target="tpu_custom_call" | custom-call | flops 1811939328 | bytes 7471104 | tf_op jit(solution)/shard_map/ffn_grad/pallas_call | solution.py:119
  170.4 1.6 collective-permute-start.75
  175.5 2.6 collective-permute-done.75
  179.1 1.6 collective-permute-start.76
  183.4 5.5 %collective-permute-done.45.last = bf16[128,768]{1,0:T(8,128)(2,1)S(1)} collective-permute-done((bf16[128,768]{1,0:T(8,128)(2,1)S(1)}, bf16[128,768]{1,0:T(8,128)(2,1)S(1)}, u32[]{:S(2)}, u32[]{:S(2)}) %collective-permute-start.45) | collective-permute-done | bytes 196640 | tf_op jit(solution)/shard_map/ppermute | solution.py:45
  189.6 2.6 first_norm_back.1
  194.1 4.6 %collective-permute-done.46.refs_1_.refs_3_ = bf16[144,768]{1,0:T(8,128)(2,1)S(1)} collective-permute-done((bf16[144,768]{1,0:T(8,128)(2,1)}, bf16[144,768]{1,0:T(8,128)(2,1)S(1)}, u32[]{:S(2)}, u32[]{:S(2)}) %collective-permute-start.46) | collective-permute-done | bytes 221216 | tf_op jit(solution)/shard_map/ppermute | solution.py:45
  201.2 2.6 prepare.1.g.refs_0_
  203.8 1.6 collective-permute-start.49
  206.0 11.8 %query_grad.1.refs_6_ = f32[3,64,512]{2,1,0:T(8,128)} custom-call(bf16[3,80,512]{2,1,0:T(8,128)(2,1)} %get-tuple-element.110.refs_7_.q, bf16[272,512]{1,0:T(8,128)(2,1)} %prepare.1.g.refs_0_, bf16[3,80,4096]{2,1,0:T(8,128)(2,1)} %get-tuple-element.155.k.refs_2_.refs_3_, bf16[3,80,4096]{2,1,0:T(8,128)(2,1)} %get-tuple-element.156.v.refs_3_.refs_4_), custom_call_target="tpu_custom_call" | custom-call | flops 4831838208 | bytes 4849664 | tf_op jit(solution)/shard_map/query_grad/pallas_call | solution.py:119
  217.8 3.9 %early_grad.1 = (bf16[192,512]{1,0:T(8,128)(2,1)}, bf16[96,384]{1,0:T(8,128)(2,1)}, bf16[96,384]{1,0:T(8,128)(2,1)}, bf16[96,384]{1,0:T(8,128)(2,1)}, bf16[96,38...) custom-call(s32[1]{0:T(128)} %constant.115.clone.1.slot.slots, ...), custom_call_target="tpu_custom_call" | custom-call | flops 301989888 | bytes 4096000 | tf_op jit(solution)/shard_map/early_grad/pallas_call | solution.py:119
  221.8 1.6 collective-permute-start.59
  223.9 4.4 %key_grad.5 = (f32[3,64,512]{2,1,0:T(8,128)}, f32[3,64,512]{2,1,0:T(8,128)}, f32[1,24,256]{2,1,0:T(8,128)}) custom-call(s32[2]{0:T(128)} %broadcast.164.slots, bf16[272,512]{1,0:T(8,128)(2,1)} %prepare.1.g.refs_0_, bf16[3,80,4096]{2,1,0:T(8,128)(2,1)} %get-tuple-element.159.refs_1_.refs_2_, bf16[3,80,4096]{2,1,0:T(8,128)(2,1)} %get-tuple-element.155.k.refs_2_.refs_3_, ...), custom_call_target="tpu_custom_call" | custom-call | flops 805306368 | bytes 6987776 | tf_op jit(solution)/shard_map/key_grad/pallas_call | solution.py:119
  228.9 3.5 %collective-permute-done.63 = bf16[48,384]{1,0:T(8,128)(2,1)S(1)} collective-permute-done((bf16[48,384]{1,0:T(8,128)(2,1)S(1)}, bf16[48,384]{1,0:T(8,128)(2,1)S(1)}, u32[]{:S(2)}, u32[]{:S(2)}) %collective-permute-start.63) | collective-permute-done | bytes 36896 | tf_op jit(solution)/shard_map/ppermute | solution.py:40
  234.6 2.6 collective-permute-done.60
  239.0 8.8 %collective-permute-done.61 = bf16[96,384]{1,0:T(8,128)(2,1)S(1)} collective-permute-done((bf16[96,384]{1,0:T(8,128)(2,1)S(1)}, bf16[96,384]{1,0:T(8,128)(2,1)S(1)}, u32[]{:S(2)}, u32[]{:S(2)}) %collective-permute-start.61) | collective-permute-done | bytes 73760 | tf_op jit(solution)/shard_map/ppermute | solution.py:35
  248.3 4.2 %collective-permute-done.65 = bf16[96,384]{1,0:T(8,128)(2,1)S(1)} collective-permute-done((bf16[96,384]{1,0:T(8,128)(2,1)S(1)}, bf16[96,384]{1,0:T(8,128)(2,1)S(1)}, u32[]{:S(2)}, u32[]{:S(2)}) %collective-permute-start.65) | collective-permute-done | bytes 73760 | tf_op jit(solution)/shard_map/ppermute | solution.py:40
  254.7 2.9 collective-permute-done.62
  261.6 6.2 %key_grad.6 = (f32[3,64,512]{2,1,0:T(8,128)}, f32[3,64,512]{2,1,0:T(8,128)}, f32[2,24,256]{2,1,0:T(8,128)}) custom-call(s32[2]{0:T(128)} %iota_multiply_fusion.slots, bf16[272,512]{1,0:T(8,128)(2,1)} %collective-permute-done.49.refs_0_, bf16[272,512]{1,0:T(8,128)(2,1)} %collective-permute-done.53.refs_1_, ...), custom_call_target="tpu_custom_call" | custom-call | flops 1610612736 | bytes 8077312 | tf_op jit(solution)/shard_map/key_grad/pallas_call | solution.py:119
  270.2 2.3 collective-permute-done.54.refs_1_
  273.6 6.0 %key_grad.7 = (f32[3,64,512]{2,1,0:T(8,128)}, f32[3,64,512]{2,1,0:T(8,128)}, f32[2,24,256]{2,1,0:T(8,128)}) custom-call(s32[2]{0:T(128)} %constant.124.clone.1.slots, bf16[272,512]{1,0:T(8,128)(2,1)} %collective-permute-done.50.refs_0_, bf16[272,512]{1,0:T(8,128)(2,1)} %collective-permute-done.54.refs_1_, ...), custom_call_target="tpu_custom_call" | custom-call | flops 1610612736 | bytes 8077312 | tf_op jit(solution)/shard_map/key_grad/pallas_call | solution.py:119
  279.7 1.8 collective-permute-start.52
  282.2 6.0 %key_grad.8 = (f32[3,64,512]{2,1,0:T(8,128)}, f32[3,64,512]{2,1,0:T(8,128)}, f32[2,24,256]{2,1,0:T(8,128)}) custom-call(s32[2]{0:T(128)} %constant.123.clone.1.slots, bf16[272,512]{1,0:T(8,128)(2,1)} %copy-done.11, bf16[272,512]{1,0:T(8,128)(2,1)} %copy-done.12, bf16[3,80,4096]{2,1,0:T(8,128)(2,1)} %get-tuple-element.159.refs_1_.refs_2_, ...), custom_call_target="tpu_custom_call" | custom-call | flops 1610612736 | bytes 8077312 | tf_op jit(solution)/shard_map/key_grad/pallas_call | solution.py:119
  288.9 4.5 %key_grad.9 = (f32[3,64,512]{2,1,0:T(8,128)}, f32[3,64,512]{2,1,0:T(8,128)}, f32[1,24,256]{2,1,0:T(8,128)}) custom-call(s32[2]{0:T(128)} %constant.122.clone.1.slots, bf16[272,256]{1,0:T(8,128)(2,1)} %copy-done.49, bf16[272,256]{1,0:T(8,128)(2,1)} %copy-done.50, bf16[3,80,4096]{2,1,0:T(8,128)(2,1)} %get-tuple-element.159.refs_1_.refs_2_, ...), custom_call_target="tpu_custom_call" | custom-call | flops 805306368 | bytes 7774208 | tf_op jit(solution)/shard_map/key_grad/pallas_call | solution.py:119
  293.4 4.4 %late_grad.1 = (bf16[256,768]{1,0:T(8,128)(2,1)}, bf16[256,768]{1,0:T(8,128)(2,1)}, bf16[96,384]{1,0:T(8,128)(2,1)}, bf16[96,384]{1,0:T(8,128)(2,1)}, bf16[96,38...) custom-call(s32[1]{0:T(128)} %constant.115.clone.1.slot.slots, ...), custom_call_target="tpu_custom_call" | custom-call | flops 754974720 | bytes 5079040 | tf_op jit(solution)/shard_map/late_grad/pallas_call | solution.py:119
  299.3 2.2 norm_total.1
  301.4 1.5 slice_reduce_fusion
  321.5 2.2 collective-permute-done.74
  324.9 1.8 collective-permute-done.58
  (368 shorter events, 90.0 us)
Async XLA Ops:
  3.0 23.5 %collective-permute-start.19 = (bf16[96,768]{1,0:T(8,128)(2,1)S(1)}, bf16[96,768]{1,0:T(8,128)(2,1)}, u32[]{:S(2)}, u32[]{:S(2)}) collective-permute-start(bf16[96,768]{1,0:T(8,128)(2,1)S(1)} %pad_maximum_fusion.5.refs_0_), channel_id=1, source_target_pairs={{0,8},{8,16},{16,24},{24,28},{28,20},{20,12},{12,4},{4,0},{1,9},{9... | collective-permute-start | bytes 442376 | tf_op jit(solution)/shard_map/ppermute | solution.py:35
  6.0 21.9 %collective-permute-start.20 = (bf16[96,768]{1,0:T(8,128)(2,1)S(1)}, bf16[96,768]{1,0:T(8,128)(2,1)}, u32[]{:S(2)}, u32[]{:S(2)}) collective-permute-start(bf16[96,768]{1,0:T(8,128)(2,1)S(1)} %pad_maximum_fusion.5.refs_0_), channel_id=1, source_target_pairs={{8,0},{16,8},{24,16},{28,24},{20,28},{12,20},{4,12},{0,4},{9,1},{1... | collective-permute-start | bytes 442376 | tf_op jit(solution)/shard_map/ppermute | solution.py:40
  6.0 6.6 %collective-permute-start = (bf16[128,768]{1,0:T(8,128)(2,1)}, bf16[128,768]{1,0:T(8,128)(2,1)S(1)}, u32[]{:S(2)}, u32[]{:S(2)}) collective-permute-start(bf16[128,768]{1,0:T(8,128)(2,1)} %tokens.1), channel_id=1, source_target_pairs={{0,2},{1,3},{2,0},{3,1},{4,6},{5,7},{6,4},{7,5},{8,10},{9,11},{10,... | collective-permute-start | bytes 589832 | tf_op jit(solution)/shard_map/ppermute | solution.py:45
  12.6 9.8 %collective-permute-start.1 = (bf16[256,768]{1,0:T(8,128)(2,1)S(1)}, bf16[256,768]{1,0:T(8,128)(2,1)S(1)}, u32[]{:S(2)}, u32[]{:S(2)}) collective-permute-start(bf16[256,768]{1,0:T(8,128)(2,1)S(1)} %constant_dynamic-update-slice_fusion.refs_0_), channel_id=1, source_target_pairs={{0,8},{8,16},{16,24},{24,28},{28,20},{20,12},{12,4},{4,0},{1,9},{9... | collective-permute-start | bytes 1179656 | tf_op jit(solution)/shard_map/ppermute | solution.py:35
  14.4 9.5 %collective-permute-start.3 = (bf16[256,768]{1,0:T(8,128)(2,1)S(1)}, bf16[256,768]{1,0:T(8,128)(2,1)S(1)}, u32[]{:S(2)}, u32[]{:S(2)}) collective-permute-start(bf16[256,768]{1,0:T(8,128)(2,1)S(1)} %constant_dynamic-update-slice_fusion.refs_0_), channel_id=1, source_target_pairs={{8,0},{16,8},{24,16},{28,24},{20,28},{12,20},{4,12},{0,4},{9,1},{1... | collective-permute-start | bytes 1179656 | tf_op jit(solution)/shard_map/ppermute | solution.py:40
  22.5 11.6 %collective-permute-start.2 = (bf16[256,768]{1,0:T(8,128)(2,1)S(1)}, bf16[256,768]{1,0:T(8,128)(2,1)S(1)}, u32[]{:S(2)}, u32[]{:S(2)}) collective-permute-start(bf16[256,768]{1,0:T(8,128)(2,1)S(1)} %collective-permute-done.1.refs_0_), channel_id=1, source_target_pairs={{0,8},{8,16},{16,24},{24,28},{28,20},{20,12},{12,4},{4,0},{1,9},{9... | collective-permute-start | bytes 1179656 | tf_op jit(solution)/shard_map/ppermute | solution.py:35
  23.9 11.0 %collective-permute-start.4 = (bf16[256,768]{1,0:T(8,128)(2,1)S(1)}, bf16[256,768]{1,0:T(8,128)(2,1)S(1)}, u32[]{:S(2)}, u32[]{:S(2)}) collective-permute-start(bf16[256,768]{1,0:T(8,128)(2,1)S(1)} %collective-permute-done.3.refs_2_), channel_id=1, source_target_pairs={{8,0},{16,8},{24,16},{28,24},{20,28},{12,20},{4,12},{0,4},{9,1},{1... | collective-permute-start | bytes 1179656 | tf_op jit(solution)/shard_map/ppermute | solution.py:40
  26.4 10.8 %collective-permute-start.21 = (bf16[96,768]{1,0:T(8,128)(2,1)}, bf16[96,768]{1,0:T(8,128)(2,1)S(1)}, u32[]{:S(2)}, u32[]{:S(2)}) collective-permute-start(bf16[96,768]{1,0:T(8,128)(2,1)} %collective-permute-done.19.refs_1_), channel_id=1, source_target_pairs={{0,8},{8,16},{16,24},{24,28},{28,20},{20,12},{12,4},{4,0},{1,9},{9... | collective-permute-start | bytes 442376 | tf_op jit(solution)/shard_map/ppermute | solution.py:35
  27.9 10.1 %collective-permute-start.22 = (bf16[96,768]{1,0:T(8,128)(2,1)}, bf16[96,768]{1,0:T(8,128)(2,1)S(1)}, u32[]{:S(2)}, u32[]{:S(2)}) collective-permute-start(bf16[96,768]{1,0:T(8,128)(2,1)} %collective-permute-done.20.refs_2_), channel_id=1, source_target_pairs={{8,0},{16,8},{24,16},{28,24},{20,28},{12,20},{4,12},{0,4},{9,1},{1... | collective-permute-start | bytes 442376 | tf_op jit(solution)/shard_map/ppermute | solution.py:40
  28.5 23.3 %collective-permute-start.27 = (bf16[256,768]{1,0:T(8,128)(2,1)S(1)}, bf16[256,768]{1,0:T(8,128)(2,1)S(1)}, u32[]{:S(2)}, u32[]{:S(2)}) collective-permute-start(bf16[256,768]{1,0:T(8,128)(2,1)S(1)} %constant_dynamic-update-slice_fusion.refs_0_), channel_id=1, source_target_pairs={{0,1},{1,0},{2,3},{3,2},{4,5},{5,4},{6,7},{7,6},{8,9},{9,8},{10,11... | collective-permute-start | bytes 1179656 | tf_op jit(solution)/shard_map/ppermute | solution.py:45
  34.1 19.4 %collective-permute-start.13 = (bf16[256,768]{1,0:T(8,128)(2,1)S(1)}, bf16[256,768]{1,0:T(8,128)(2,1)S(1)}, u32[]{:S(2)}, u32[]{:S(2)}) collective-permute-start(bf16[256,768]{1,0:T(8,128)(2,1)S(1)} %collective-permute-done.2.refs_0_), channel_id=1, source_target_pairs={{0,8},{8,16},{16,24},{24,28},{28,20},{20,12},{12,4},{4,0},{1,9},{9... | collective-permute-start | bytes 1179656 | tf_op jit(solution)/shard_map/ppermute | solution.py:35
  34.9 18.7 %collective-permute-start.15 = (bf16[256,768]{1,0:T(8,128)(2,1)S(1)}, bf16[256,768]{1,0:T(8,128)(2,1)S(1)}, u32[]{:S(2)}, u32[]{:S(2)}) collective-permute-start(bf16[256,768]{1,0:T(8,128)(2,1)S(1)} %collective-permute-done.4.refs_2_), channel_id=1, source_target_pairs={{8,0},{16,8},{24,16},{28,24},{20,28},{12,20},{4,12},{0,4},{9,1},{1... | collective-permute-start | bytes 1179656 | tf_op jit(solution)/shard_map/ppermute | solution.py:40
  37.2 9.2 %collective-permute-start.23 = (bf16[96,768]{1,0:T(8,128)(2,1)S(1)}, bf16[96,768]{1,0:T(8,128)(2,1)S(1)}, u32[]{:S(2)}, u32[]{:S(2)}) collective-permute-start(bf16[96,768]{1,0:T(8,128)(2,1)S(1)} %collective-permute-done.21.refs_3_), channel_id=1, source_target_pairs={{0,8},{8,16},{16,24},{24,28},{28,20},{20,12},{12,4},{4,0},{1,9},{9... | collective-permute-start | bytes 442376 | tf_op jit(solution)/shard_map/ppermute | solution.py:35
  38.1 9.3 %collective-permute-start.24 = (bf16[96,768]{1,0:T(8,128)(2,1)S(1)}, bf16[96,768]{1,0:T(8,128)(2,1)S(1)}, u32[]{:S(2)}, u32[]{:S(2)}) collective-permute-start(bf16[96,768]{1,0:T(8,128)(2,1)S(1)} %collective-permute-done.22.refs_4_), channel_id=1, source_target_pairs={{8,0},{16,8},{24,16},{28,24},{20,28},{12,20},{4,12},{0,4},{9,1},{1... | collective-permute-start | bytes 442376 | tf_op jit(solution)/shard_map/ppermute | solution.py:40
  50.9 5.6 %collective-permute-start.32 = (bf16[256,768]{1,0:T(8,128)(2,1)S(1)}, bf16[256,768]{1,0:T(8,128)(2,1)S(1)}, u32[]{:S(2)}, u32[]{:S(2)}) collective-permute-start(bf16[256,768]{1,0:T(8,128)(2,1)S(1)} %collective-permute-done.1.refs_0_), channel_id=1, source_target_pairs={{0,1},{1,0},{2,3},{3,2},{4,5},{5,4},{6,7},{7,6},{8,9},{9,8},{10,11... | collective-permute-start | bytes 1179656 | tf_op jit(solution)/shard_map/ppermute | solution.py:45
  51.8 5.2 %collective-permute-start.33 = (bf16[256,768]{1,0:T(8,128)(2,1)S(1)}, bf16[256,768]{1,0:T(8,128)(2,1)S(1)}, u32[]{:S(2)}, u32[]{:S(2)}) collective-permute-start(bf16[256,768]{1,0:T(8,128)(2,1)S(1)} %collective-permute-done.3.refs_2_), channel_id=1, source_target_pairs={{0,1},{1,0},{2,3},{3,2},{4,5},{5,4},{6,7},{7,6},{8,9},{9,8},{10,11... | collective-permute-start | bytes 1179656 | tf_op jit(solution)/shard_map/ppermute | solution.py:45
  51.8 13.0 %collective-permute-start.5 = (bf16[96,2304]{1,0:T(8,128)(2,1)S(1)}, bf16[96,2304]{1,0:T(8,128)(2,1)S(1)}, u32[]{:S(2)}, u32[]{:S(2)}) collective-permute-start(bf16[96,2304]{1,0:T(8,128)(2,1)S(1)} %pad_maximum_fusion.1.refs_0_), channel_id=1, source_target_pairs={{0,8},{8,16},{16,24},{24,28},{28,20},{20,12},{12,4},{4,0},{1,9},{9... | collective-permute-start | bytes 1327112 | tf_op jit(solution)/shard_map/ppermute | solution.py:35
  53.7 5.5 %collective-permute-start.31 = (bf16[256,768]{1,0:T(8,128)(2,1)S(1)}, bf16[256,768]{1,0:T(8,128)(2,1)S(1)}, u32[]{:S(2)}, u32[]{:S(2)}) collective-permute-start(bf16[256,768]{1,0:T(8,128)(2,1)S(1)} %collective-permute-done.4.refs_2_), channel_id=1, source_target_pairs={{0,1},{1,0},{2,3},{3,2},{4,5},{5,4},{6,7},{7,6},{8,9},{9,8},{10,11... | collective-permute-start | bytes 1179656 | tf_op jit(solution)/shard_map/ppermute | solution.py:45
  56.5 31.5 %collective-permute-start.6 = (bf16[96,2304]{1,0:T(8,128)(2,1)S(1)}, bf16[96,2304]{1,0:T(8,128)(2,1)}, u32[]{:S(2)}, u32[]{:S(2)}) collective-permute-start(bf16[96,2304]{1,0:T(8,128)(2,1)S(1)} %pad_maximum_fusion.1.refs_0_), channel_id=1, source_target_pairs={{8,0},{16,8},{24,16},{28,24},{20,28},{12,20},{4,12},{0,4},{9,1},{1... | collective-permute-start | bytes 1327112 | tf_op jit(solution)/shard_map/ppermute | solution.py:40
  57.0 18.0 %collective-permute-start.14 = (bf16[128,768]{1,0:T(8,128)(2,1)}, bf16[128,768]{1,0:T(8,128)(2,1)S(1)}, u32[]{:S(2)}, u32[]{:S(2)}) collective-permute-start(bf16[128,768]{1,0:T(8,128)(2,1)} %slice.166), channel_id=1, source_target_pairs={{0,8},{8,16},{16,24},{24,28},{28,20},{20,12},{12,4},{4,0},{1,9},{9... | collective-permute-start | bytes 589832 | tf_op jit(solution)/shard_map/ppermute | solution.py:35
  58.6 16.5 %collective-permute-start.16 = (bf16[128,768]{1,0:T(8,128)(2,1)}, bf16[128,768]{1,0:T(8,128)(2,1)S(1)}, u32[]{:S(2)}, u32[]{:S(2)}) collective-permute-start(bf16[128,768]{1,0:T(8,128)(2,1)} %slice.167), channel_id=1, source_target_pairs={{8,0},{16,8},{24,16},{28,24},{20,28},{12,20},{4,12},{0,4},{9,1},{1... | collective-permute-start | bytes 589832 | tf_op jit(solution)/shard_map/ppermute | solution.py:40
  59.2 30.4 %collective-permute-start.28 = (bf16[256,768]{1,0:T(8,128)(2,1)S(1)}, bf16[256,768]{1,0:T(8,128)(2,1)S(1)}, u32[]{:S(2)}, u32[]{:S(2)}) collective-permute-start(bf16[256,768]{1,0:T(8,128)(2,1)S(1)} %collective-permute-done.13.refs_0_), channel_id=1, source_target_pairs={{0,1},{1,0},{2,3},{3,2},{4,5},{5,4},{6,7},{7,6},{8,9},{9,8},{10,11... | collective-permute-start | bytes 1179656 | tf_op jit(solution)/shard_map/ppermute | solution.py:45
  64.8 25.4 %collective-permute-start.29 = (bf16[256,768]{1,0:T(8,128)(2,1)S(1)}, bf16[256,768]{1,0:T(8,128)(2,1)S(1)}, u32[]{:S(2)}, u32[]{:S(2)}) collective-permute-start(bf16[256,768]{1,0:T(8,128)(2,1)S(1)} %collective-permute-done.15.refs_2_), channel_id=1, source_target_pairs={{0,1},{1,0},{2,3},{3,2},{4,5},{5,4},{6,7},{7,6},{8,9},{9,8},{10,11... | collective-permute-start | bytes 1179656 | tf_op jit(solution)/shard_map/ppermute | solution.py:45
  75.0 22.2 %collective-permute-start.17 = (bf16[128,768]{1,0:T(8,128)(2,1)S(1)}, bf16[128,768]{1,0:T(8,128)(2,1)S(1)}, u32[]{:S(2)}, u32[]{:S(2)}) collective-permute-start(bf16[128,768]{1,0:T(8,128)(2,1)S(1)} %collective-permute-done.14.refs_0_), channel_id=1, source_target_pairs={{0,1},{1,0},{2,3},{3,2},{4,5},{5,4},{6,7},{7,6},{8,9},{9,8},{10,11... | collective-permute-start | bytes 589832 | tf_op jit(solution)/shard_map/ppermute | solution.py:45
  75.1 22.1 %collective-permute-start.18 = (bf16[128,768]{1,0:T(8,128)(2,1)S(1)}, bf16[128,768]{1,0:T(8,128)(2,1)S(1)}, u32[]{:S(2)}, u32[]{:S(2)}) collective-permute-start(bf16[128,768]{1,0:T(8,128)(2,1)S(1)} %collective-permute-done.16.refs_1_), channel_id=1, source_target_pairs={{0,1},{1,0},{2,3},{3,2},{4,5},{5,4},{6,7},{7,6},{8,9},{9,8},{10,11... | collective-permute-start | bytes 589832 | tf_op jit(solution)/shard_map/ppermute | solution.py:45
  87.9 16.0 %collective-permute-start.7 = (bf16[96,2304]{1,0:T(8,128)(2,1)S(1)}, bf16[96,2304]{1,0:T(8,128)(2,1)S(1)}, u32[]{:S(2)}, u32[]{:S(2)}) collective-permute-start(bf16[96,2304]{1,0:T(8,128)(2,1)S(1)} %copy-done.69), channel_id=1, source_target_pairs={{0,8},{8,16},{16,24},{24,28},{28,20},{20,12},{12,4},{4,0},{1,9},{9... | collective-permute-start | bytes 1327112 | tf_op jit(solution)/shard_map/ppermute | solution.py:35
  89.6 16.1 %collective-permute-start.8 = (bf16[96,2304]{1,0:T(8,128)(2,1)}, bf16[96,2304]{1,0:T(8,128)(2,1)}, u32[]{:S(2)}, u32[]{:S(2)}) collective-permute-start(bf16[96,2304]{1,0:T(8,128)(2,1)} %collective-permute-done.6.refs_2_), channel_id=1, source_target_pairs={{8,0},{16,8},{24,16},{28,24},{20,28},{12,20},{4,12},{0,4},{9,1},{1... | collective-permute-start | bytes 1327112 | tf_op jit(solution)/shard_map/ppermute | solution.py:40
  104.0 14.5 %collective-permute-start.9 = (bf16[96,2304]{1,0:T(8,128)(2,1)S(1)}, bf16[96,2304]{1,0:T(8,128)(2,1)S(1)}, u32[]{:S(2)}, u32[]{:S(2)}) collective-permute-start(bf16[96,2304]{1,0:T(8,128)(2,1)S(1)} %collective-permute-done.7.refs_3_), channel_id=1, source_target_pairs={{0,8},{8,16},{16,24},{24,28},{28,20},{20,12},{12,4},{4,0},{1,9},{9... | collective-permute-start | bytes 1327112 | tf_op jit(solution)/shard_map/ppermute | solution.py:35
  105.6 14.5 %collective-permute-start.10 = (bf16[96,2304]{1,0:T(8,128)(2,1)}, bf16[96,2304]{1,0:T(8,128)(2,1)S(1)}, u32[]{:S(2)}, u32[]{:S(2)}) collective-permute-start(bf16[96,2304]{1,0:T(8,128)(2,1)} %collective-permute-done.8.refs_4_), channel_id=1, source_target_pairs={{8,0},{16,8},{24,16},{28,24},{20,28},{12,20},{4,12},{0,4},{9,1},{1... | collective-permute-start | bytes 1327112 | tf_op jit(solution)/shard_map/ppermute | solution.py:40
  107.2 6.8 %collective-permute-start.35 = (bf16[128,768]{1,0:T(8,128)(2,1)S(1)}, bf16[128,768]{1,0:T(8,128)(2,1)S(1)}, u32[]{:S(2)}, u32[]{:S(2)}) collective-permute-start(bf16[128,768]{1,0:T(8,128)(2,1)S(1)} %add_convert_fusion.9), channel_id=1, source_target_pairs={{0,2},{1,3},{2,0},{3,1},{4,6},{5,7},{6,4},{7,5},{8,10},{9,11},{10,... | collective-permute-start | bytes 589832 | tf_op jit(solution)/shard_map/ppermute | solution.py:45
  116.9 6.1 %collective-permute-start.36 = (bf16[128,768]{1,0:T(8,128)(2,1)}, bf16[128,768]{1,0:T(8,128)(2,1)S(1)}, u32[]{:S(2)}, u32[]{:S(2)}) collective-permute-start(bf16[128,768]{1,0:T(8,128)(2,1)} %get-tuple-element.138.refs_9_.refs_0_), channel_id=1, source_target_pairs={{0,2},{1,3},{2,0},{3,1},{4,6},{5,7},{6,4},{7,5},{8,10},{9,11},{10,... | collective-permute-start | bytes 589832 | tf_op jit(solution)/shard_map/ppermute | solution.py:45
  118.5 6.2 %collective-permute-start.11 = (bf16[48,2304]{1,0:T(8,128)(2,1)S(1)}, bf16[48,2304]{1,0:T(8,128)(2,1)S(1)}, u32[]{:S(2)}, u32[]{:S(2)}) collective-permute-start(bf16[48,2304]{1,0:T(8,128)(2,1)S(1)} %slice.164), channel_id=1, source_target_pairs={{0,8},{8,16},{16,24},{24,28},{28,20},{20,12},{12,4},{4,0},{1,9},{9... | collective-permute-start | bytes 663560 | tf_op jit(solution)/shard_map/ppermute | solution.py:35
  120.2 6.5 %collective-permute-start.12 = (bf16[48,2304]{1,0:T(8,128)(2,1)S(1)}, bf16[48,2304]{1,0:T(8,128)(2,1)S(1)}, u32[]{:S(2)}, u32[]{:S(2)}) collective-permute-start(bf16[48,2304]{1,0:T(8,128)(2,1)S(1)} %slice.165), channel_id=1, source_target_pairs={{8,0},{16,8},{24,16},{28,24},{20,28},{12,20},{4,12},{0,4},{9,1},{1... | collective-permute-start | bytes 663560 | tf_op jit(solution)/shard_map/ppermute | solution.py:40
  121.1 5.5 %collective-permute-start.37 = (bf16[128,768]{1,0:T(8,128)(2,1)}, bf16[128,768]{1,0:T(8,128)(2,1)S(1)}, u32[]{:S(2)}, u32[]{:S(2)}) collective-permute-start(bf16[128,768]{1,0:T(8,128)(2,1)} %get-tuple-element.138.refs_9_.refs_0_), channel_id=1, source_target_pairs={{0,1},{1,0},{2,3},{3,2},{4,5},{5,4},{6,7},{7,6},{8,9},{9,8},{10,11... | collective-permute-start | bytes 589832 | tf_op jit(solution)/shard_map/ppermute | solution.py:45
  138.1 7.0 %collective-permute-start.40 = (bf16[128,768]{1,0:T(8,128)(2,1)S(1)}, bf16[128,768]{1,0:T(8,128)(2,1)S(1)}, u32[]{:S(2)}, u32[]{:S(2)}) collective-permute-start(bf16[128,768]{1,0:T(8,128)(2,1)S(1)} %add_convert_fusion.8), channel_id=1, source_target_pairs={{0,2},{1,3},{2,0},{3,1},{4,6},{5,7},{6,4},{7,5},{8,10},{9,11},{10,... | collective-permute-start | bytes 589832 | tf_op jit(solution)/shard_map/ppermute | solution.py:45
  148.5 6.3 %collective-permute-start.41 = (bf16[128,768]{1,0:T(8,128)(2,1)}, bf16[128,768]{1,0:T(8,128)(2,1)S(1)}, u32[]{:S(2)}, u32[]{:S(2)}) collective-permute-start(bf16[128,768]{1,0:T(8,128)(2,1)} %get-tuple-element.143.refs_0_.refs_4_), channel_id=1, source_target_pairs={{0,2},{1,3},{2,0},{3,1},{4,6},{5,7},{6,4},{7,5},{8,10},{9,11},{10,... | collective-permute-start | bytes 589832 | tf_op jit(solution)/shard_map/ppermute | solution.py:45
  149.1 6.5 %collective-permute-start.42 = (bf16[128,768]{1,0:T(8,128)(2,1)}, bf16[128,768]{1,0:T(8,128)(2,1)S(1)}, u32[]{:S(2)}, u32[]{:S(2)}) collective-permute-start(bf16[128,768]{1,0:T(8,128)(2,1)} %get-tuple-element.143.refs_0_.refs_4_), channel_id=1, source_target_pairs={{0,1},{1,0},{2,3},{3,2},{4,5},{5,4},{6,7},{7,6},{8,9},{9,8},{10,11... | collective-permute-start | bytes 589832 | tf_op jit(solution)/shard_map/ppermute | solution.py:45
  170.4 7.7 %collective-permute-start.75 = (bf16[48,2304]{1,0:T(8,128)(2,1)}, bf16[48,2304]{1,0:T(8,128)(2,1)S(1)}, u32[]{:S(2)}, u32[]{:S(2)}) collective-permute-start(bf16[48,2304]{1,0:T(8,128)(2,1)} %get-tuple-element.193), channel_id=1, source_target_pairs={{0,8},{8,16},{16,24},{24,28},{28,20},{20,12},{12,4},{4,0},{1,9},{9... | collective-permute-start | bytes 663560 | tf_op jit(solution)/shard_map/ppermute | solution.py:35
  173.1 9.1 %collective-permute-start.44 = (bf16[256,768]{1,0:T(8,128)(2,1)S(1)}, bf16[256,768]{1,0:T(8,128)(2,1)S(1)}, u32[]{:S(2)}, u32[]{:S(2)}) collective-permute-start(bf16[256,768]{1,0:T(8,128)(2,1)S(1)} %copy-done.71), channel_id=1, source_target_pairs={{0,1},{1,0},{2,3},{3,2},{4,5},{5,4},{6,7},{7,6},{8,9},{9,8},{10,11... | collective-permute-start | bytes 1179656 | tf_op jit(solution)/shard_map/ppermute | solution.py:45
  174.1 8.1 %collective-permute-start.79 = (bf16[48,2304]{1,0:T(8,128)(2,1)}, bf16[48,2304]{1,0:T(8,128)(2,1)S(1)}, u32[]{:S(2)}, u32[]{:S(2)}) collective-permute-start(bf16[48,2304]{1,0:T(8,128)(2,1)} %get-tuple-element.198), channel_id=1, source_target_pairs={{8,0},{16,8},{24,16},{28,24},{20,28},{12,20},{4,12},{0,4},{9,1},{1... | collective-permute-start | bytes 663560 | tf_op jit(solution)/shard_map/ppermute | solution.py:40
  179.1 13.6 %collective-permute-start.76 = (bf16[96,2304]{1,0:T(8,128)(2,1)S(1)}, bf16[96,2304]{1,0:T(8,128)(2,1)S(1)}, u32[]{:S(2)}, u32[]{:S(2)}) collective-permute-start(bf16[96,2304]{1,0:T(8,128)(2,1)S(1)} %pad_maximum_fusion.2), channel_id=1, source_target_pairs={{0,8},{8,16},{16,24},{24,28},{28,20},{20,12},{12,4},{4,0},{1,9},{9... | collective-permute-start | bytes 1327112 | tf_op jit(solution)/shard_map/ppermute | solution.py:35
  182.3 6.6 %collective-permute-start.45 = (bf16[128,768]{1,0:T(8,128)(2,1)S(1)}, bf16[128,768]{1,0:T(8,128)(2,1)S(1)}, u32[]{:S(2)}, u32[]{:S(2)}) collective-permute-start(bf16[128,768]{1,0:T(8,128)(2,1)S(1)} %add_convert_fusion.7), channel_id=1, source_target_pairs={{0,2},{1,3},{2,0},{3,1},{4,6},{5,7},{6,4},{7,5},{8,10},{9,11},{10,... | collective-permute-start | bytes 589832 | tf_op jit(solution)/shard_map/ppermute | solution.py:45
  182.9 15.8 %collective-permute-start.80 = (bf16[96,2304]{1,0:T(8,128)(2,1)S(1)}, bf16[96,2304]{1,0:T(8,128)(2,1)}, u32[]{:S(2)}, u32[]{:S(2)}) collective-permute-start(bf16[96,2304]{1,0:T(8,128)(2,1)S(1)} %pad_maximum_fusion.3), channel_id=1, source_target_pairs={{8,0},{16,8},{24,16},{28,24},{20,28},{12,20},{4,12},{0,4},{9,1},{1... | collective-permute-start | bytes 1327112 | tf_op jit(solution)/shard_map/ppermute | solution.py:40
  192.2 6.5 %collective-permute-start.46 = (bf16[144,768]{1,0:T(8,128)(2,1)}, bf16[144,768]{1,0:T(8,128)(2,1)S(1)}, u32[]{:S(2)}, u32[]{:S(2)}) collective-permute-start(bf16[144,768]{1,0:T(8,128)(2,1)} %get-tuple-element.152.refs_0_.refs_2_), channel_id=1, source_target_pairs={{0,2},{1,3},{2,0},{3,1},{4,6},{5,7},{6,4},{7,5},{8,10},{9,11},{10,... | collective-permute-start | bytes 663560 | tf_op jit(solution)/shard_map/ppermute | solution.py:45
  192.7 7.7 %collective-permute-start.47 = (bf16[144,768]{1,0:T(8,128)(2,1)}, bf16[144,768]{1,0:T(8,128)(2,1)S(1)}, u32[]{:S(2)}, u32[]{:S(2)}) collective-permute-start(bf16[144,768]{1,0:T(8,128)(2,1)} %get-tuple-element.152.refs_0_.refs_2_), channel_id=1, source_target_pairs={{0,1},{1,0},{2,3},{3,2},{4,5},{5,4},{6,7},{7,6},{8,9},{9,8},{10,11... | collective-permute-start | bytes 663560 | tf_op jit(solution)/shard_map/ppermute | solution.py:45
  192.9 40.8 %collective-permute-start.77 = (bf16[96,2304]{1,0:T(8,128)(2,1)S(1)}, bf16[96,2304]{1,0:T(8,128)(2,1)S(1)}, u32[]{:S(2)}, u32[]{:S(2)}) collective-permute-start(bf16[96,2304]{1,0:T(8,128)(2,1)S(1)} %add_convert_fusion.3), channel_id=1, source_target_pairs={{0,8},{8,16},{16,24},{24,28},{28,20},{20,12},{12,4},{4,0},{1,9},{9... | collective-permute-start | bytes 1327112 | tf_op jit(solution)/shard_map/ppermute | solution.py:35
  199.9 53.4 %collective-permute-start.81 = (bf16[96,2304]{1,0:T(8,128)(2,1)S(1)}, bf16[96,2304]{1,0:T(8,128)(2,1)S(1)}, u32[]{:S(2)}, u32[]{:S(2)}) collective-permute-start(bf16[96,2304]{1,0:T(8,128)(2,1)S(1)} %add_convert_fusion.1), channel_id=1, source_target_pairs={{8,0},{16,8},{24,16},{28,24},{20,28},{12,20},{4,12},{0,4},{9,1},{1... | collective-permute-start | bytes 1327112 | tf_op jit(solution)/shard_map/ppermute | solution.py:40
  203.8 55.7 %collective-permute-start.49 = (bf16[272,512]{1,0:T(8,128)(2,1)}, bf16[272,512]{1,0:T(8,128)(2,1)}, u32[]{:S(2)}, u32[]{:S(2)}) collective-permute-start(bf16[272,512]{1,0:T(8,128)(2,1)} %prepare.1.g.refs_0_), channel_id=1, source_target_pairs={{0,8},{8,16},{16,24},{24,28},{28,20},{20,12},{12,4},{4,0},{1,9},{9... | collective-permute-start | bytes 835592 | tf_op jit(solution)/shard_map/ppermute | solution.py:35
  205.4 55.1 %collective-permute-start.53 = (bf16[272,512]{1,0:T(8,128)(2,1)}, bf16[272,512]{1,0:T(8,128)(2,1)}, u32[]{:S(2)}, u32[]{:S(2)}) collective-permute-start(bf16[272,512]{1,0:T(8,128)(2,1)} %prepare.1.g.refs_0_), channel_id=1, source_target_pairs={{8,0},{16,8},{24,16},{28,24},{20,28},{12,20},{4,12},{0,4},{9,1},{1... | collective-permute-start | bytes 835592 | tf_op jit(solution)/shard_map/ppermute | solution.py:40
  221.8 6.6 %collective-permute-start.59 = (bf16[48,384]{1,0:T(8,128)(2,1)}, bf16[48,384]{1,0:T(8,128)(2,1)S(1)}, u32[]{:S(2)}, u32[]{:S(2)}) collective-permute-start(bf16[48,384]{1,0:T(8,128)(2,1)} %get-tuple-element.173), channel_id=1, source_target_pairs={{0,8},{8,16},{16,24},{24,28},{28,20},{20,12},{12,4},{4,0},{1,9},{9... | collective-permute-start | bytes 110600 | tf_op jit(solution)/shard_map/ppermute | solution.py:35
  237.2 30.5 %collective-permute-start.78 = (bf16[96,2304]{1,0:T(8,128)(2,1)S(1)}, bf16[96,2304]{1,0:T(8,128)(2,1)S(1)}, u32[]{:S(2)}, u32[]{:S(2)}) collective-permute-start(bf16[96,2304]{1,0:T(8,128)(2,1)S(1)} %add_convert_fusion.2), channel_id=1, source_target_pairs={{0,8},{8,16},{16,24},{24,28},{28,20},{20,12},{12,4},{4,0},{1,9},{9... | collective-permute-start | bytes 1327112 | tf_op jit(solution)/shard_map/ppermute | solution.py:35
  238.5 9.3 %collective-permute-start.61 = (bf16[96,384]{1,0:T(8,128)(2,1)S(1)}, bf16[96,384]{1,0:T(8,128)(2,1)S(1)}, u32[]{:S(2)}, u32[]{:S(2)}) collective-permute-start(bf16[96,384]{1,0:T(8,128)(2,1)S(1)} %add_convert_fusion.17), channel_id=1, source_target_pairs={{0,8},{8,16},{16,24},{24,28},{28,20},{20,12},{12,4},{4,0},{1,9},{9... | collective-permute-start | bytes 221192 | tf_op jit(solution)/shard_map/ppermute | solution.py:35
  252.5 5.1 %collective-permute-start.62 = (bf16[96,384]{1,0:T(8,128)(2,1)S(1)}, bf16[96,384]{1,0:T(8,128)(2,1)S(1)}, u32[]{:S(2)}, u32[]{:S(2)}) collective-permute-start(bf16[96,384]{1,0:T(8,128)(2,1)S(1)} %add_convert_fusion.16), channel_id=1, source_target_pairs={{0,8},{8,16},{16,24},{24,28},{28,20},{20,12},{12,4},{4,0},{1,9},{9... | collective-permute-start | bytes 221192 | tf_op jit(solution)/shard_map/ppermute | solution.py:35
  253.4 5.3 %collective-permute-start.66 = (bf16[96,384]{1,0:T(8,128)(2,1)S(1)}, bf16[96,384]{1,0:T(8,128)(2,1)S(1)}, u32[]{:S(2)}, u32[]{:S(2)}) collective-permute-start(bf16[96,384]{1,0:T(8,128)(2,1)S(1)} %add_convert_fusion.14), channel_id=1, source_target_pairs={{8,0},{16,8},{24,16},{28,24},{20,28},{12,20},{4,12},{0,4},{9,1},{1... | collective-permute-start | bytes 221192 | tf_op jit(solution)/shard_map/ppermute | solution.py:40
  257.6 10.1 %collective-permute-start.82 = (bf16[96,2304]{1,0:T(8,128)(2,1)S(1)}, bf16[96,2304]{1,0:T(8,128)(2,1)S(1)}, u32[]{:S(2)}, u32[]{:S(2)}) collective-permute-start(bf16[96,2304]{1,0:T(8,128)(2,1)S(1)} %add_convert_fusion), channel_id=1, source_target_pairs={{8,0},{16,8},{24,16},{28,24},{20,28},{12,20},{4,12},{0,4},{9,1},{1... | collective-permute-start | bytes 1327112 | tf_op jit(solution)/shard_map/ppermute | solution.py:40
  259.5 9.6 %collective-permute-start.50 = (bf16[272,512]{1,0:T(8,128)(2,1)}, bf16[272,512]{1,0:T(8,128)(2,1)}, u32[]{:S(2)}, u32[]{:S(2)}) collective-permute-start(bf16[272,512]{1,0:T(8,128)(2,1)} %collective-permute-done.49.refs_0_), channel_id=1, source_target_pairs={{0,8},{8,16},{16,24},{24,28},{28,20},{20,12},{12,4},{4,0},{1,9},{9... | collective-permute-start | bytes 835592 | tf_op jit(solution)/shard_map/ppermute | solution.py:35
  260.5 11.9 %collective-permute-start.54 = (bf16[272,512]{1,0:T(8,128)(2,1)}, bf16[272,512]{1,0:T(8,128)(2,1)}, u32[]{:S(2)}, u32[]{:S(2)}) collective-permute-start(bf16[272,512]{1,0:T(8,128)(2,1)} %collective-permute-done.53.refs_1_), channel_id=1, source_target_pairs={{8,0},{16,8},{24,16},{28,24},{20,28},{12,20},{4,12},{0,4},{9,1},{1... | collective-permute-start | bytes 835592 | tf_op jit(solution)/shard_map/ppermute | solution.py:40
  269.2 10.5 %collective-permute-start.51 = (bf16[272,512]{1,0:T(8,128)(2,1)}, bf16[272,512]{1,0:T(8,128)(2,1)S(1)}, u32[]{:S(2)}, u32[]{:S(2)}) collective-permute-start(bf16[272,512]{1,0:T(8,128)(2,1)} %collective-permute-done.50.refs_0_), channel_id=1, source_target_pairs={{0,8},{8,16},{16,24},{24,28},{28,20},{20,12},{12,4},{4,0},{1,9},{9... | collective-permute-start | bytes 835592 | tf_op jit(solution)/shard_map/ppermute | solution.py:35
  272.4 9.1 %collective-permute-start.55 = (bf16[272,512]{1,0:T(8,128)(2,1)}, bf16[272,512]{1,0:T(8,128)(2,1)S(1)}, u32[]{:S(2)}, u32[]{:S(2)}) collective-permute-start(bf16[272,512]{1,0:T(8,128)(2,1)} %collective-permute-done.54.refs_1_), channel_id=1, source_target_pairs={{8,0},{16,8},{24,16},{28,24},{20,28},{12,20},{4,12},{0,4},{9,1},{1... | collective-permute-start | bytes 835592 | tf_op jit(solution)/shard_map/ppermute | solution.py:40
  279.7 8.5 %collective-permute-start.52 = (bf16[272,256]{1,0:T(8,128)(2,1)S(1)}, bf16[272,256]{1,0:T(8,128)(2,1)S(1)}, u32[]{:S(2)}, u32[]{:S(2)}) collective-permute-start(bf16[272,256]{1,0:T(8,128)(2,1)S(1)} %slice.173), channel_id=1, source_target_pairs={{0,8},{8,16},{16,24},{24,28},{28,20},{20,12},{12,4},{4,0},{1,9},{9... | collective-permute-start | bytes 417800 | tf_op jit(solution)/shard_map/ppermute | solution.py:35
  281.5 6.7 %collective-permute-start.56 = (bf16[272,256]{1,0:T(8,128)(2,1)S(1)}, bf16[272,256]{1,0:T(8,128)(2,1)S(1)}, u32[]{:S(2)}, u32[]{:S(2)}) collective-permute-start(bf16[272,256]{1,0:T(8,128)(2,1)S(1)} %slice.174), channel_id=1, source_target_pairs={{8,0},{16,8},{24,16},{28,24},{20,28},{12,20},{4,12},{0,4},{9,1},{1... | collective-permute-start | bytes 417800 | tf_op jit(solution)/shard_map/ppermute | solution.py:40
  297.8 7.3 %collective-permute-start.67 = (bf16[48,384]{1,0:T(8,128)(2,1)}, bf16[48,384]{1,0:T(8,128)(2,1)S(1)}, u32[]{:S(2)}, u32[]{:S(2)}) collective-permute-start(bf16[48,384]{1,0:T(8,128)(2,1)} %get-tuple-element.182), channel_id=1, source_target_pairs={{0,8},{8,16},{16,24},{24,28},{28,20},{20,12},{12,4},{4,0},{1,9},{9... | collective-permute-start | bytes 110600 | tf_op jit(solution)/shard_map/ppermute | solution.py:35
  305.1 14.9 %collective-permute-start.57 = (bf16[256,768]{1,0:T(8,128)(2,1)}, bf16[256,768]{1,0:T(8,128)(2,1)S(1)}, u32[]{:S(2)}, u32[]{:S(2)}) collective-permute-start(bf16[256,768]{1,0:T(8,128)(2,1)} %get-tuple-element.171), channel_id=1, source_target_pairs={{0,1},{1,0},{2,3},{3,2},{4,5},{5,4},{6,7},{7,6},{8,9},{9,8},{10,11... | collective-permute-start | bytes 1179656 | tf_op jit(solution)/shard_map/ppermute | solution.py:45
  321.0 5.7 %collective-permute-start.58 = (bf16[128,768]{1,0:T(8,128)(2,1)S(1)}, bf16[128,768]{1,0:T(8,128)(2,1)S(1)}, u32[]{:S(2)}, u32[]{:S(2)}) collective-permute-start(bf16[128,768]{1,0:T(8,128)(2,1)S(1)} %add_convert_fusion.6), channel_id=1, source_target_pairs={{0,2},{1,3},{2,0},{3,1},{4,6},{5,7},{6,4},{7,5},{8,10},{9,11},{10,... | collective-permute-start | bytes 589832 | tf_op jit(solution)/shard_map/ppermute | solution.py:45
  (97 other events, 992.9 us)
